TPU v7x, 32 devices: a whole 2x2x4 slice. The times are simulated.
32 devices in a mesh: ctx: 4 (over y, x), vis: 8 (over z, core).
Axes of the slice: x: 2, y: 2, z: 4, core: 2. Of those that a mesh axis runs over, the one named last changes fastest.
Arguments:
- patches: bfloat16 [4096, 1280], P(('ctx', 'vis')), may hold values from -10 to 10
- vis_gain: float32 [1280], replicated, may hold values from 0.5 to 1.5
- w_qkv: bfloat16 [1280, 3840], P(None, 'vis'), may hold values from -2 to 2
- w_out: bfloat16 [1280, 1280], P('vis'), may hold values from -0.15625 to 0.15625
- merge_gain: float32 [1280], replicated, may hold values from 0.5 to 1.5
- w_merge: bfloat16 [5120, 8192], P(None, 'vis'), may hold values from -0.078125 to 0.078125
- token_dest: int32 [4, 256], replicated, may hold values from 0 to 3, as said below
- token_row: int32 [4, 256], replicated, may hold values from 0 to 1023, as said below
- prompt_text: bfloat16 [4096, 8192], P('ctx', 'vis'), may hold values from -6 to 6
- kv_gain: float32 [8192], P('vis'), may hold values from 0.5 to 1.5
- w_kv: bfloat16 [8192, 1024], P('vis'), may hold values from -1 to 1
- queries: bfloat16 [512, 4096], P('ctx'), may hold values from -12 to 12
- resp_kv: bfloat16 [512, 1024], P('ctx'), may hold values from -12 to 12
- resp_len: int32 [4], P('ctx'), may hold values from 64 to 128
Outputs:
- attended: bfloat16 [512, 4096], P('ctx')
Inputs may be any that keep to these rules, and one draw needn't show every extreme that they name: `token_dest`: the tokens of one image are in order of their prompt shard; at most 96 tokens of one image go to one shard, and from every image exactly 96 go to some shard. `token_row`: no two visual tokens take the same position of one shard.
All inputs are finite; a program needn't handle non-finite values.
Results may differ from a plain program's by a relative error of at most 0.014.
Values may be sent and summed in bfloat16 or wider, within the bound.
A program may use at most 128 MiB of HBM per device.

v0:
```python
import math

import jax
import jax.numpy as jnp
from jax import lax
from jax.sharding import PartitionSpec as P

VD = 1280
VHEADS = 16
D = 8192
HD = 128
QH = 32
KVH = 4
VHD = 80
MD = 5120


EPS = 1e-06


def merged_2(shard, axis, combine):
    everything = jax.tree.map(lambda part: lax.all_gather(part, axis), shard)
    initial = jax.tree.map(lambda part: part[0], everything)

    def lap(k, so_far):
        return combine(so_far, jax.tree.map(lambda part: part[k], everything))

    return lax.fori_loop(1, lax.axis_size(axis), lap, initial)


def layer_norm(values, gain):
    center = values - jnp.mean(values, axis=-1, keepdims=True)
    spread = jnp.mean(center * center, axis=-1, keepdims=True)
    return center * lax.rsqrt(spread + EPS) * gain


def dense_attention(query, keys, values):
    count = query.shape[0]
    block = min(512, count)
    scale = 1.0 / math.sqrt(query.shape[1])

    def one_block(part):
        scores = jnp.dot(part, keys.T, preferred_element_type=jnp.float32) * scale
        highest = jnp.max(scores, axis=1, keepdims=True)
        expo = jnp.exp(scores - highest)
        summed = jnp.sum(expo, axis=1, keepdims=True)
        mixed = jnp.dot(expo.astype(jnp.bfloat16), values, preferred_element_type=jnp.float32)
        return (mixed / summed).astype(jnp.bfloat16)

    blocks = query.reshape(count // block, block, query.shape[1])
    return lax.map(one_block, blocks).reshape(count, values.shape[1])


def head_attention(packed):
    stacked = jnp.transpose(packed, (1, 0, 2))

    def one_head(item):
        return dense_attention(item[:, :VHD], item[:, VHD : 2 * VHD], item[:, 2 * VHD :])

    return jnp.transpose(lax.map(one_head, stacked), (1, 0, 2))


def combine_partial(first, second):
    highest = jnp.maximum(first[0], second[0])
    fade_one = jnp.exp(first[0] - highest)
    fade_two = jnp.exp(second[0] - highest)
    return (
        highest,
        first[1] * fade_one + second[1] * fade_two,
        first[2] * fade_one[..., None] + second[2] * fade_two[..., None],
    )


def per_device(
    patches,
    vis_gain,
    w_qkv,
    w_out,
    merge_gain,
    w_merge,
    token_dest,
    token_row,
    prompt_text,
    kv_gain,
    w_kv,
    queries,
    resp_kv,
    resp_len,
):
    ctx_count = lax.axis_size("ctx")
    vis_count = lax.axis_size("vis")
    ctx_index = lax.axis_index("ctx")
    vis_index = lax.axis_index("vis")
    patch_count = patches.shape[0]
    floats = patches.astype(jnp.float32)
    normed = layer_norm(floats, vis_gain).astype(jnp.bfloat16)
    local_heads = VHEADS // vis_count
    qkv = jnp.dot(
        lax.all_gather(normed, "vis", axis=0, tiled=True), w_qkv, preferred_element_type=jnp.float32
    ).astype(jnp.bfloat16)
    image_rows = qkv.shape[0]
    heads = head_attention(qkv.reshape(image_rows, local_heads, 3 * VHD))
    returned = lax.all_to_all(heads, "vis", split_axis=0, concat_axis=1, tiled=True).reshape(
        patch_count, VD
    )
    projected = jnp.dot(
        returned,
        lax.all_gather(w_out, "vis", axis=0, tiled=True),
        preferred_element_type=jnp.float32,
    )
    mixed = floats + projected
    merged = layer_norm(mixed, merge_gain).astype(jnp.bfloat16).reshape(patch_count // 4, MD)
    visual = jnp.dot(
        lax.all_gather(merged, "vis", axis=0, tiled=True),
        w_merge,
        preferred_element_type=jnp.float32,
    ).astype(jnp.bfloat16)
    image_tokens = visual.shape[0]
    capacity = 3 * (image_tokens // ctx_count) // 2
    slots = jnp.arange(capacity, dtype=jnp.int32)
    shard_rows = prompt_text.shape[0]
    own_dest = lax.dynamic_index_in_dim(token_dest, ctx_index, 0, keepdims=False)
    shards = jnp.arange(ctx_count, dtype=jnp.int32)
    counts_out = jnp.sum((own_dest[None, :] == shards[:, None]).astype(jnp.int32), axis=1)
    starts_out = jnp.cumsum(counts_out) - counts_out
    picks = jnp.clip(starts_out[:, None] + slots[None, :], 0, image_tokens - 1).reshape(-1)
    filled = (slots[None, :] < counts_out[:, None]).reshape(-1, 1)
    outgoing = jnp.take(visual, picks, axis=0)
    outgoing = jnp.where(filled, outgoing, jnp.zeros_like(outgoing)).reshape(
        ctx_count, capacity, -1
    )
    arrived = lax.all_to_all(outgoing, "ctx", split_axis=0, concat_axis=0, tiled=True)
    pool = arrived.reshape(ctx_count * capacity, -1)
    firsts = jnp.sum((token_dest < ctx_index).astype(jnp.int32), axis=1)
    counts_in = jnp.sum((token_dest == ctx_index).astype(jnp.int32), axis=1)
    lookup = jnp.clip(firsts[:, None] + slots[None, :], 0, image_tokens - 1)
    places = jnp.take_along_axis(token_row, lookup, axis=1)
    live = slots[None, :] < counts_in[:, None]
    targets = jnp.where(live, places, shard_rows).reshape(-1)
    numbers = jnp.arange(ctx_count * capacity, dtype=jnp.int32) + 1
    source = jnp.zeros((shard_rows,), jnp.int32).at[targets].set(numbers, mode="drop")
    incoming = jnp.take(pool, jnp.maximum(source - 1, 0), axis=0)
    prompt = jnp.where((source > 0)[:, None], incoming, prompt_text)
    prompt_floats = prompt.astype(jnp.float32)
    squares = lax.psum(jnp.sum(prompt_floats * prompt_floats, axis=1), "vis")
    inverse = lax.rsqrt(squares / D + EPS)
    scaled = (prompt_floats * inverse[:, None] * kv_gain).astype(jnp.bfloat16)
    kv_share = lax.psum_scatter(
        jnp.dot(scaled, w_kv, preferred_element_type=jnp.float32),
        "vis",
        scatter_dimension=0,
        tiled=True,
    ).astype(jnp.bfloat16)
    width = KVH * HD
    group = QH // KVH
    resp_rows = queries.shape[0]
    scale = 1.0 / math.sqrt(HD)
    q_heads = queries.reshape(resp_rows, KVH, group, HD)

    def update(state, keys, values, visible):
        highest, summed, weighted = state
        scores = (
            jnp.einsum("rkgd,nkd->kgrn", q_heads, keys, preferred_element_type=jnp.float32) * scale
        )
        if visible is not None:
            scores = jnp.where(visible, scores, -1e30)
        new_high = jnp.maximum(highest, jnp.max(scores, axis=3))
        expo = jnp.exp(scores - new_high[..., None])
        if visible is not None:
            expo = jnp.where(visible, expo, 0.0)
        fade = jnp.exp(highest - new_high)
        summed = summed * fade + jnp.sum(expo, axis=3)
        weighted = weighted * fade[..., None] + jnp.einsum(
            "kgrn,nkd->kgrd", expo.astype(jnp.bfloat16), values, preferred_element_type=jnp.float32
        )
        return (new_high, summed, weighted)

    def fold_block(state, piece):
        count = piece.shape[0]
        return update(
            state,
            piece[:, :width].reshape(count, KVH, HD),
            piece[:, width:].reshape(count, KVH, HD),
            None,
        )

    def fold_prompt(state, piece):
        count = piece.shape[0]
        if count > 512 and count % 512 == 0:
            blocks = piece.reshape(count // 512, 512, 2 * width)

            def scan_step(inner, block):
                return (fold_block(inner, block), None)

            state, unused = lax.scan(scan_step, state, blocks)
            return state
        return fold_block(state, piece)

    own_count = resp_rows // vis_count
    own = lax.dynamic_slice_in_dim(resp_kv, vis_index * own_count, own_count, 0)
    key_positions = vis_index * own_count + jnp.arange(own_count, dtype=jnp.int32)
    query_positions = jnp.arange(resp_rows, dtype=jnp.int32)
    own_visible = key_positions[None, :] <= query_positions[:, None]
    start_state = (
        jnp.full((KVH, group, resp_rows), -1e30, jnp.float32),
        jnp.zeros((KVH, group, resp_rows), jnp.float32),
        jnp.zeros((KVH, group, resp_rows, HD), jnp.float32),
    )
    state = update(
        start_state,
        own[:, :width].reshape(own_count, KVH, HD),
        own[:, width:].reshape(own_count, KVH, HD),
        own_visible,
    )
    state = fold_prompt(state, lax.all_gather(kv_share, "ctx", axis=0, tiled=True))
    highest, summed, weighted = merged_2(state, "vis", combine_partial)
    result = weighted / summed[..., None]
    result = jnp.transpose(result, (2, 0, 1, 3)).reshape(resp_rows, QH * HD)
    live = (query_positions < resp_len[0])[:, None]
    return jnp.where(live, result, 0.0).astype(jnp.bfloat16)


def solution(mesh):
    return jax.shard_map(
        per_device,
        mesh=mesh,
        in_specs=(
            P(("ctx", "vis"), None),
            P(),
            P(None, "vis"),
            P("vis", None),
            P(),
            P(None, "vis"),
            P(),
            P(),
            P("ctx", "vis"),
            P("vis"),
            P("vis", None),
            P("ctx", None),
            P("ctx", None),
            P("ctx"),
        ),
        out_specs=P("ctx", None),
        check_vma=False,
    )
```

profile of v0, /device:TPU:0, one launch (start us, length us, event | category | flops | bytes accessed | tf_op | source)
XLA Modules:
  0.0 479.5 jit_solution(3582567656449933819)
XLA Ops:
  11.8 35.8 %all-gather.7.cloned.1.call-done = bf16[1024,1280]{1,0:T(8,128)(2,1)} async-done(((bf16[128,1280]{1,0:T(8,128)(2,1)}), bf16[1024,1280]{1,0:T(8,128)(2,1)}) %all-gather.7.cloned.1.call-update) | async-done | bytes 2621456 | tf_op jit(solution)/shard_map/all_gather | solution.py:99
  52.4 11.1 %while.40 = (s32[]{:T(128)}, bf16[2,1024,80]{2,1,0:T(8,128)(2,1)}, bf16[2,1024,240]{2,1,0:T(8,128)(2,1)}, s32[]{:T(128)}, s32[]{:T(128)}, /*index=5*/s32[]{:T(128)}) while((s32[]{:T(128)}, bf16[2,1024,80]{2,1,0:T(8,128)(2,1)}, bf16[2,1024,240]{2,1,0:T(8,128)(2,1)}, s32[]{:T(128)}, s32[]{:T(128)}, /*index=5*/s32[]{:T(128)}) %tuple.93), condition=%wide.region_13.14_spmd, body=%wide.region_8.0_spmd.sunk | while | flops 172047360 | bytes 9758946 | solution.py:60
  65.1 31.0 %all_to_all.20 = bf16[1024,2,80]{2,1,0:T(2,128)(2,1)S(1)} all-to-all(bf16[1024,2,80]{2,1,0:T(2,128)(2,1)S(1)} %bitcast.150), channel_id=1, replica_groups=mesh['ctx'=4,'vis'=8] {'vis'}, dimensions={0} | all-to-all | bytes 655360 | tf_op jit(solution)/shard_map/all_to_all | solution.py:103
  103.9 31.7 %all-gather.11.cloned.1.call-done = bf16[256,5120]{1,0:T(8,128)(2,1)} async-done(((bf16[32,5120]{1,0:T(8,128)(2,1)}), bf16[256,5120]{1,0:T(8,128)(2,1)}) %all-gather.11.cloned.1.call-update) | async-done | bytes 2621456 | tf_op jit(solution)/shard_map/all_gather | solution.py:114
  135.6 7.6 %convolution_convert_fusion.1 = bf16[256,1024]{1,0:T(8,128)(2,1)S(1)} fusion(bf16[256,5120]{1,0:T(8,128)(2,1)} %all-gather.11.cloned.1.call-done, bf16[5120,1024]{1,0:T(8,128)(2,1)} %param.25), kind=kOutput, calls=%fused_computation.52 | convolution fusion | flops 2684616704 | bytes 13631488 | tf_op jit(solution)/shard_map/dot_general | solution.py:113
  159.0 4.0 all-to-all-done.1
  163.1 5.4 %gather_fusion.1 = bf16[1024,1024]{1,0:T(8,128)(2,1)} fusion(bf16[384,1024]{1,0:T(8,128)(2,1)S(1)} %bitcast.141, s32[1024]{0:T(1024)S(1)} %fusion.55), kind=kCustom, calls=%fused_computation.1 | custom fusion | bytes 4198400 | tf_op jit(solution)/shard_map/jit(_take)/gather | solution.py:142
  168.4 4.1 fusion.19
  172.5 13.9 %psum.7 = f32[1024]{0:T(1024)S(1)} all-reduce(f32[1024]{0:T(1024)S(1)} %get-tuple-element.265), channel_id=1, replica_groups=mesh['ctx'=4,'vis'=8] {'vis'}, use_global_device_ids=true, to_apply=%region_17.18 | all-reduce | flops 1024 | bytes 8192 | tf_op jit(solution)/shard_map/psum | solution.py:145
  186.4 5.9 %fusion.26 = f32[1024,1024]{1,0:T(8,128)} fusion(bf16[1024,1024]{1,0:T(8,128)(2,1)S(1)} %copy-done, bf16[1024,1024]{1,0:T(8,128)(2,1)} %get-tuple-element.266, f32[1024]{0:T(1024)S(1)} %copy-done.5, f32[1024]{0:T(1024)S(1)} %add_rsqrt_fusion), kind=kOutput, calls=%fused_computation.43 | convolution fusion | flops 2151677952 | bytes 8396800 | tf_op jit(solution)/shard_map/dot_general | solution.py:149
  192.4 47.3 %reduce-scatter.2.cloned.1.call-done = f32[128,1024]{1,0:T(8,128)} async-done(((f32[1024,1024]{1,0:T(8,128)}), f32[128,1024]{1,0:T(8,128)}) %reduce-scatter.2.cloned.1.call-update) | async-done | bytes 524304 | tf_op jit(solution)/shard_map/reduce_scatter | solution.py:148
  244.3 22.3 %all-gather.13.cloned.1.call-done = bf16[512,1024]{1,0:T(8,128)(2,1)} async-done(((bf16[128,1024]{1,0:T(8,128)(2,1)}), bf16[512,1024]{1,0:T(8,128)(2,1)}) %all-gather.13.cloned.1.call-update) | async-done | bytes 1048592 | tf_op jit(solution)/shard_map/all_gather | solution.py:215
  270.8 5.5 %bitcast_reduce_fusion = (f32[4,8,128]{2,1,0:T(8,128)S(1)}, f32[4,512,128,8]{2,1,3,0:T(8,128)}) fusion(bf16[128,4,8,128]{3,2,1,0:T(8,128)(2,1)S(1)} %bitcast.145, bf16[512,4,128,1]{2,1,0,3:T(4,128)(2,1)} %bitcast.148), kind=kOutput, calls=%fused_computation.30 | convolution fusion | flops 541061120 | bytes 9977856 | tf_op jit(solution)/shard_map/rkgd,nkd->kgrn/dot_general | solution.py:163
  277.6 5.4 %fusion.22 = f32[4,8,128,128]{3,2,1,0:T(8,128)S(1)} fusion(f32[4,512,128,8]{2,1,3,0:T(8,128)} %get-tuple-element.289, f32[4,8,128]{2,1,0:T(8,128)S(1)} %get-tuple-element.277, bf16[512,4,128,1]{2,1,0,3:T(4,128)(2,1)S(1)} %bitcast.152), kind=kOutput, calls=%fused_computation.39 | convolution fusion | flops 543162368 | bytes 11026432 | tf_op jit(solution)/shard_map/kgrn,nkd->kgrd/dot_general | solution.py:173
  286.3 4.8 %fusion.18 = f32[4,8,128]{2,1,0:T(8,128)S(1)} fusion(f32[4,512,128,8]{2,1,3,0:T(8,128)} %get-tuple-element.289, f32[4,8,128]{2,1,0:T(8,128)S(1)} %get-tuple-element.277), kind=kLoop, calls=%fused_computation.33 | loop fusion | flops 6287360 | bytes 8421376 | tf_op jit(solution)/shard_map/reduce_sum | solution.py:172
  291.2 14.7 %all_gather.30 = f32[8,4,8,128]{3,2,1,0:T(8,128)S(1)} all-gather(f32[1,4,8,128]{3,2,1,0:T(8,128)S(1)} %get-tuple-element.279), channel_id=1, replica_groups=mesh['ctx'=4,'vis'=8] {'vis'}, dimensions={0}, use_global_device_ids=true | all-gather | bytes 147456 | tf_op jit(solution)/shard_map/all_gather | solution.py:22
  305.8 21.1 %all_gather.31 = f32[8,4,8,128]{3,2,1,0:T(8,128)S(1)} all-gather(f32[1,4,8,128]{3,2,1,0:T(8,128)S(1)} %get-tuple-element.278), channel_id=1, replica_groups=mesh['ctx'=4,'vis'=8] {'vis'}, dimensions={0}, use_global_device_ids=true | all-gather | bytes 147456 | tf_op jit(solution)/shard_map/all_gather | solution.py:22
  326.9 111.4 %all-gather.15.cloned.1.call-done = f32[32,8,128,128]{3,2,1,0:T(8,128)} async-done(((f32[4,8,128,128]{3,2,1,0:T(8,128)}), f32[32,8,128,128]{3,2,1,0:T(8,128)}) %all-gather.15.cloned.1.call-update) | async-done | bytes 16777232 | tf_op jit(solution)/shard_map/all_gather | solution.py:22
  441.5 27.0 %while.41 = (s32[]{:T(128)}, f32[4,8,128]{2,1,0:T(8,128)S(1)}, f32[4,8,128]{2,1,0:T(8,128)S(1)}, f32[4,8,128,128]{3,2,1,0:T(8,128)}, f32[8,4,8,128]{3,2,1,0:T(8,...) while((s32[]{:T(128)}, f32[4,8,128]{2,1,0:T(8,128)S(1)}, ...), condition=%wide.region_23.24_spmd, body=%wide.region_22.23_spmd.sunk | while | flops 1597445 | bytes 6455447 | solution.py:28
  441.5 3.8 fusion.93
  445.4 3.8 fusion.93
  449.2 3.8 fusion.93
  457.0 3.8 fusion.93
  460.8 3.8 fusion.93
  (124 shorter events, 80.5 us)
Async XLA Ops:
  6.5 179.9 %copy-start = (bf16[1024,1024]{1,0:T(8,128)(2,1)S(1)}, bf16[1024,1024]{1,0:T(8,128)(2,1)}, u32[]{:S(2)}) copy-start(bf16[1024,1024]{1,0:T(8,128)(2,1)} %param.30) | copy-start | bytes 6291460
  6.5 41.0 %all-gather.7.cloned.1.call-start = ((), (), s32[]{:S(2)}) async-start(), calls=%async_computation.3 | async-start | bytes 2949120 | tf_op jit(solution)/shard_map/all_gather | solution.py:99
  11.0 87.9 %all-gather.9.cloned.1.call-start = ((), (), s32[]{:S(2)}) async-start(), calls=%async_computation.4 | async-start | bytes 3686400 | tf_op jit(solution)/shard_map/all_gather | solution.py:108
  11.7 123.8 %all-gather.11.cloned.1.call-start = ((), (), s32[]{:S(2)}) async-start(), calls=%async_computation.5 | async-start | bytes 2949120 | tf_op jit(solution)/shard_map/all_gather | solution.py:114
  63.5 35.4 %copy-start.2 = (bf16[128,1280]{1,0:T(8,128)(2,1)S(1)}, bf16[128,1280]{1,0:T(8,128)(2,1)}, u32[]{:S(2)}) copy-start(bf16[128,1280]{1,0:T(8,128)(2,1)} %param.20) | copy-start | bytes 983044
  98.9 2.9 copy-start.3
  101.6 1.4 copy-start.4
  145.9 6.3 %copy-start.1 = (s32[4,256]{1,0:T(4,128)S(1)}, s32[4,256]{1,0:T(4,128)}, u32[]{:S(2)}) copy-start(s32[4,256]{1,0:T(4,128)} %param.27) | copy-start | bytes 12292
  148.1 15.0 %all-to-all-start.1 = ((bf16[4,96,1024]{2,1,0:T(8,128)(2,1)}), bf16[4,96,1024]{2,1,0:T(8,128)(2,1)S(1)}, u32[]{:S(2)}, u32[]{:S(2)}) async-start(bf16[4,96,1024]{2,1,0:T(8,128)(2,1)} %select_select_fusion.1), calls=%async_computation.1 | async-start | bytes 1572864 | tf_op jit(solution)/shard_map/all_to_all | solution.py:132
  151.8 88.0 %reduce-scatter.2.cloned.1.call-start = ((), (), s32[]{:S(2)}) async-start(), calls=%async_computation.6 | async-start | bytes 4718592 | tf_op jit(solution)/shard_map/reduce_scatter | solution.py:148
  168.4 18.0 %copy-start.5 = (f32[1024]{0:T(1024)S(1)}, f32[1024]{0:T(1024)}, u32[]{:S(2)}) copy-start(f32[1024]{0:T(1024)} %param.29) | copy-start | bytes 12292
  192.4 74.3 %all-gather.13.cloned.1.call-start = ((), (), s32[]{:S(2)}) async-start(), calls=%async_computation.7 | async-start | bytes 1310720 | tf_op jit(solution)/shard_map/all_gather | solution.py:215
  241.5 196.8 %all-gather.15.cloned.1.call-start = ((), (), s32[]{:S(2)}) async-start(), calls=%async_computation.8 | async-start | bytes 18874368 | tf_op jit(solution)/shard_map/all_gather | solution.py:22
Sparse Core Ops, SparseCore 0:
  11.1 36.4 all-gather.6
  49.2 49.6 all-gather.8
  103.1 32.4 all-gather.10
  192.5 47.1 reduce-scatter.1
  241.6 24.9 all-gather.12
  285.7 152.5 all-gather.14
where the time goes:
time: 480 us; the launch traced here: 479 us
  waiting for transfers between devices  256 us (53%)
  blocking collectives  80.7 us (17%)
  other arithmetic  51.2 us (11%)
  matrix products  38.1 us (8%)
  local copies, waits for them, and re-layouts  35.4 us (7%)
  between operations  14.4 us (3%)
    all_gather x1, waiting for transfers between devices, merged_2(): everything = jax.tree.map(lambda part: lax.all_gather(part, axis), shard)  111 us
    reduce_scatter x1, waiting for transfers between devices, per_device(): lax.psum_scatter(jnp.dot(scaled, w_kv, preferred_element_type=jnp.float32...  47.3 us
    all_gather x2, blocking collectives, merged_2(): everything = jax.tree.map(lambda part: lax.all_gather(part, axis), shard)  35.8 us
    all_gather x1, waiting for transfers between devices, per_device(): lax.all_gather(normed, 'vis', axis=0, tiled=True)  35.8 us
    all_gather x1, waiting for transfers between devices, per_device(): lax.all_gather(merged, 'vis', axis=0, tiled=True)  31.7 us
    all_to_all x1, blocking collectives, per_device(): lax.all_to_all(heads, 'vis', split_axis=0, concat_axis=1, tiled=True)  31 us
    add x7, other arithmetic, combine_partial(): first[2] * fade_one[..., None] + second[2] * fade_two[..., None]  26.9 us
    all_gather x1, waiting for transfers between devices, per_device(): lax.all_gather(kv_share, 'ctx', axis=0, tiled=True)  22.3 us
  transfers between devices with their start and end apart: 7, of which 7 were waited for; matrix products, arithmetic and copies ran while one was open for 7% of the time, Pallas kernels for 0%

commit v1 on v0

v1 whole, which is shorter than its diff:
```python
import math

import jax
import jax.numpy as jnp
from jax import lax
from jax.sharding import Mesh, PartitionSpec as P

VD = 1280
VHEADS = 16
D = 8192
HD = 128
QH = 32
KVH = 4
VHD = 80
MD = 5120


EPS = 1e-06
VIS = ("vk", "vg")
F32 = jnp.float32
BF16 = jnp.bfloat16


def layer_norm(values, gain):
    center = values - jnp.mean(values, axis=-1, keepdims=True)
    spread = jnp.mean(center * center, axis=-1, keepdims=True)
    return center * lax.rsqrt(spread + EPS) * gain


def vision_attention(qkv, local_heads):
    scale = 1.0 / math.sqrt(VHD)
    outs = []
    for h in range(local_heads):
        base = h * 3 * VHD
        query = qkv[:, base : base + VHD]
        keys = qkv[:, base + VHD : base + 2 * VHD]
        values = qkv[:, base + 2 * VHD : base + 3 * VHD]
        scores = jnp.einsum("qd,kd->qk", query, keys, preferred_element_type=F32) * scale
        expo = jnp.exp(scores - jnp.max(scores, axis=1, keepdims=True))
        summed = jnp.sum(expo, axis=1, keepdims=True)
        mixed = jnp.dot(expo.astype(BF16), values, preferred_element_type=F32)
        outs.append((mixed / summed).astype(BF16))
    return jnp.concatenate(outs, axis=1)


def partial_kv(rows, weight, heads, parts):
    count = rows.shape[0]
    raw = jnp.dot(rows, weight, preferred_element_type=F32)
    floats = rows.astype(F32)
    squares = jnp.sum(floats * floats, axis=1)
    each = count // parts
    pieces = raw.reshape(parts, each, 2, heads, HD).transpose(3, 0, 1, 2, 4)
    pieces = pieces.reshape(heads * parts, each, 2 * HD)
    extra = squares.reshape(parts, each // HD // 2 if each >= 2 * HD else 1, -1)
    extra = jnp.pad(extra, ((0, 0), (0, 8 - extra.shape[1]), (0, 2 * HD - extra.shape[2])))
    extra = jnp.broadcast_to(extra[None], (heads,) + extra.shape).reshape(heads * parts, 8, 2 * HD)
    return jnp.concatenate([pieces, extra], axis=1)


def whole_kv(partial, count):
    total = lax.psum_scatter(partial, VIS, scatter_dimension=0, tiled=True)[0]
    each = total.shape[0] - 8
    rows = each // HD // 2 if each >= 2 * HD else 1
    squares = total[each : each + rows, : each // rows].reshape(each)
    inverse = lax.rsqrt(squares / D + EPS)
    share = (total[:each] * inverse[:, None]).astype(BF16)
    return lax.all_gather(share, ("ctx", "vg"), axis=0, tiled=True)


def per_device(
    patches,
    vis_gain,
    w_qkv,
    w_out,
    merge_gain,
    w_merge,
    token_dest,
    token_row,
    prompt_text,
    kv_gain,
    w_kv,
    queries,
    resp_kv,
    resp_len,
):
    vis_count = lax.axis_size("vk") * lax.axis_size("vg")
    parts = lax.axis_size("vg")
    ctx_count = lax.axis_size("ctx")
    vis_index = lax.axis_index("vk") * parts + lax.axis_index("vg")
    patch_count = patches.shape[0]
    shard_rows = prompt_text.shape[0]
    local_heads = VHEADS // vis_count

    floats = patches.astype(F32)
    normed = layer_norm(floats, vis_gain).astype(BF16)
    gathered = lax.all_gather(normed, VIS, axis=0, tiled=True)
    w_out_all = lax.all_gather(w_out, VIS, axis=0, tiled=True)

    weight = (w_kv.astype(F32) * kv_gain[:, None]).astype(BF16)
    text_kv = whole_kv(partial_kv(prompt_text, weight, KVH, parts), shard_rows)

    qkv = jnp.dot(gathered, w_qkv, preferred_element_type=F32).astype(BF16)
    heads = vision_attention(qkv, local_heads)
    returned = lax.all_to_all(heads, VIS, split_axis=0, concat_axis=1, tiled=True)
    projected = jnp.dot(returned, w_out_all, preferred_element_type=F32)
    mixed = floats + projected
    merged = layer_norm(mixed, merge_gain).astype(BF16).reshape(patch_count // 4, MD)
    visual = jnp.dot(
        lax.all_gather(merged, VIS, axis=0, tiled=True), w_merge, preferred_element_type=F32
    ).astype(BF16)
    image_kv = whole_kv(partial_kv(visual, weight, KVH, parts), visual.shape[0])

    flat = (token_dest * shard_rows + token_row).reshape(-1)
    positions = jnp.arange(ctx_count * shard_rows, dtype=jnp.int32)
    taken = jnp.any(positions[:, None] == flat[None, :], axis=1)

    width = KVH * HD
    group = QH // KVH
    mine = QH // vis_count
    resp_rows = queries.shape[0]
    scale = 1.0 / math.sqrt(HD)
    query = lax.dynamic_slice_in_dim(queries, vis_index * mine * HD, mine * HD, 1)
    query = query.reshape(resp_rows, mine, HD).transpose(1, 0, 2).reshape(mine * resp_rows, HD)
    kv_head = (vis_index * mine) // group
    own_keys = lax.dynamic_slice_in_dim(resp_kv, kv_head * HD, HD, 1)
    own_values = lax.dynamic_slice_in_dim(resp_kv, width + kv_head * HD, HD, 1)
    early_keys = jnp.concatenate([text_kv[:, :HD], own_keys], axis=0)
    early_values = jnp.concatenate([text_kv[:, HD:], own_values], axis=0)
    query_positions = jnp.arange(resp_rows, dtype=jnp.int32)
    causal = query_positions[None, :] <= query_positions[:, None]
    visible = jnp.concatenate(
        [jnp.broadcast_to(~taken[None, :], (resp_rows, taken.shape[0])), causal], axis=1
    )
    visible = jnp.broadcast_to(visible[None], (mine,) + visible.shape).reshape(
        mine * resp_rows, -1
    )

    def scores_of(keys):
        return jnp.einsum("qd,kd->qk", query, keys, preferred_element_type=F32) * scale

    scores = jnp.where(visible, scores_of(early_keys), -1e30)
    early_high = jnp.max(scores, axis=1, keepdims=True)
    expo = jnp.where(visible, jnp.exp(scores - early_high), 0.0)
    early_sum = jnp.sum(expo, axis=1, keepdims=True)
    early_mix = jnp.dot(expo.astype(BF16), early_values, preferred_element_type=F32)

    late_scores = scores_of(image_kv[:, :HD])
    high = jnp.maximum(early_high, jnp.max(late_scores, axis=1, keepdims=True))
    late = jnp.exp(late_scores - high)
    fade = jnp.exp(early_high - high)
    summed = early_sum * fade + jnp.sum(late, axis=1, keepdims=True)
    mix = early_mix * fade + jnp.dot(
        late.astype(BF16), image_kv[:, HD:], preferred_element_type=F32
    )
    live = jnp.tile(query_positions < resp_len[0], mine)[:, None]
    result = jnp.where(live, mix / summed, 0.0).astype(BF16)
    result = result.reshape(mine, resp_rows, HD)
    whole = lax.all_gather(result, VIS, axis=0, tiled=True)
    return whole.transpose(1, 0, 2).reshape(resp_rows, QH * HD)


def solution(mesh):
    ctx_count, vis_count = mesh.shape["ctx"], mesh.shape["vis"]
    parts = max(1, vis_count // KVH)
    fine = Mesh(mesh.devices.reshape(ctx_count, vis_count // parts, parts), ("ctx", "vk", "vg"))
    return jax.shard_map(
        per_device,
        mesh=fine,
        in_specs=(
            P(("ctx",) + VIS, None),
            P(),
            P(None, VIS),
            P(VIS, None),
            P(),
            P(None, VIS),
            P(),
            P(),
            P("ctx", VIS),
            P(VIS),
            P(VIS, None),
            P("ctx", None),
            P("ctx", None),
            P("ctx"),
        ),
        out_specs=P("ctx", None),
        check_vma=False,
    )
```

time: 480 us -> 289 us (0.60)
  waiting for transfers between devices: 256 us -> 160 us
  blocking collectives: 80.7 us -> 32.8 us
  other arithmetic: 51.2 us -> 25.2 us
  local copies, waits for them, and re-layouts: 35.4 us -> 26.4 us
  matrix products: 38.1 us -> 29.6 us
    all_gather x5, waiting for transfers between devices: 204 us -> 83.6 us  [the longest x1 27.4 us: per_device(): lax.all_gather(merged, VIS, axis=0, tiled=True)]
    reduce_scatter x1 -> x2, waiting for transfers between devices: 47.3 us -> 75.2 us  [whole_kv(): total = lax.psum_scatter(partial, VIS, scatter_dimension=0, tiled=True)[0]]
    add x17 -> x1, other arithmetic: 27 us -> 0.01 us  [per_device(): summed = early_sum * fade + jnp.sum(late, axis=1, keepdims=True)]
    all_gather x2 -> x1, blocking collectives: 35.8 us -> 9.78 us  [whole_kv(): return lax.all_gather(share, ('ctx', 'vg'), axis=0, tiled=True)]
    reshape x6 -> x8, local copies, waits for them, and re-layouts: 5.38 us -> 20.6 us  [the longest x3 12.1 us: partial_kv(): pieces = raw.reshape(parts, each, 2, heads, HD).transpose(3, 0, 1, 2, 4)]
    psum x1 -> x0, blocking collectives: 13.9 us -> none  [per_device(): squares = lax.psum(jnp.sum(prompt_floats * prompt_floats, axis=1), 'vis')]
    gather x4 -> x0, local copies, waits for them, and re-layouts: 11.8 us -> none  [the longest x1 5.36 us: per_device(): incoming = jnp.take(pool, jnp.maximum(source - 1, 0), axis=0)]
    dot_general x16 -> x13, matrix products: 38.1 us -> 29.6 us  [the longest x1 7.86 us: per_device(): jnp.dot(lax.all_gather(merged, VIS, axis=0, tiled=True), w_merge, preferr...]
  transfers between devices with their start and end apart: 7 -> 7, of which waited for: 7 -> 7; matrix products, arithmetic and copies ran while one was open for 7% -> 24% of each run, Pallas kernels for 0% -> 0%
where the time goes in v1:
time: 289 us
  waiting for transfers between devices  160 us (55%)
  blocking collectives  32.8 us (11%)
  matrix products  29.6 us (10%)
  local copies, waits for them, and re-layouts  26.4 us (9%)
  other arithmetic  25.2 us (9%)
  between operations  14.5 us (5%)
    reduce_scatter x2, waiting for transfers between devices, whole_kv(): total = lax.psum_scatter(partial, VIS, scatter_dimension=0, tiled=True)[0]  75.2 us
    all_gather x1, waiting for transfers between devices, per_device(): lax.all_gather(merged, VIS, axis=0, tiled=True)  27.4 us
    all_to_all x1, blocking collectives, per_device(): lax.all_to_all(heads, VIS, split_axis=0, concat_axis=1, tiled=True)  23 us
    all_gather x1, waiting for transfers between devices, per_device(): whole = lax.all_gather(result, VIS, axis=0, tiled=True)  19.6 us
    all_gather x1, waiting for transfers between devices, per_device(): w_out_all = lax.all_gather(w_out, VIS, axis=0, tiled=True)  16.1 us
    all_gather x1, waiting for transfers between devices, whole_kv(): return lax.all_gather(share, ('ctx', 'vg'), axis=0, tiled=True)  15.4 us
    reshape x3, local copies, waits for them, and re-layouts, partial_kv(): pieces = raw.reshape(parts, each, 2, heads, HD).transpose(3, 0, 1, 2, 4)  12.1 us
    all_gather x1, blocking collectives, whole_kv(): return lax.all_gather(share, ('ctx', 'vg'), axis=0, tiled=True)  9.78 us
  transfers between devices with their start and end apart: 7, of which 7 were waited for; matrix products, arithmetic and copies ran while one was open for 24% of the time, Pallas kernels for 0%

profile of v1, /device:TPU:0, one launch (start us, length us, event | category | flops | bytes accessed | tf_op | source)
XLA Modules:
  0.0 288.6 jit_solution(13425192446473688497)
XLA Ops:
  9.0 1.9 fusion.42
  11.7 2.1 multiply_reduce_fusion
  13.8 6.9 %convolution_bitcast_fusion = f32[1024,1024]{0,1:T(8,128)} fusion(bf16[1024,1024]{1,0:T(8,128)(2,1)} %param.22, bf16[1024,1024]{1,0:T(8,128)(2,1)} %param.24, f32[1024]{0:T(1024)} %param.23), kind=kOutput, calls=%fused_computation.19 | convolution fusion | flops 2150629376 | bytes 8392704 | tf_op jit(solution)/shard_map/dot_general | solution.py:48
  20.7 6.6 %reshape.149 = f32[2,512,2,4,128]{1,0,4,3,2:T(2,128)} reshape(f32[1024,1024]{0,1:T(8,128)} %convolution_bitcast_fusion) | data formatting | bytes 8388608 | tf_op jit(solution)/shard_map/reshape | solution.py:52
  27.3 5.0 %copy.66 = f32[2,512,2,4,128]{1,4,2,0,3:T(8,128)} copy(f32[2,512,2,4,128]{1,0,4,3,2:T(2,128)} %reshape.149) | data formatting | bytes 8388608 | tf_op jit(solution)/shard_map/reshape | solution.py:52
  32.3 5.4 %copy.67 = f32[8,512,256]{2,1,0:T(8,128)} copy(f32[8,512,256]{1,2,0:T(8,128)} %bitcast.70) | data formatting | bytes 8388608 | tf_op jit(solution)/shard_map/reshape | solution.py:53
  37.7 4.6 %pad_maximum_fusion = f32[8,520,256]{2,1,0:T(8,128)} fusion(f32[8,8,256]{2,1,0:T(8,128)S(1)} %bitcast.77, f32[8,512,256]{2,1,0:T(8,128)} %copy.67), kind=kLoop, calls=%fused_computation.6 | loop fusion | flops 1064960 | bytes 8519680 | tf_op jit(solution)/shard_map/concatenate | solution.py:57
  42.3 5.2 %all-gather.8.cloned.1.call-done = bf16[1024,1280]{1,0:T(8,128)(2,1)} async-done(((bf16[128,1280]{1,0:T(8,128)(2,1)}), bf16[1024,1280]{1,0:T(8,128)(2,1)}) %all-gather.8.cloned.1.call-update) | async-done | bytes 2621456 | tf_op jit(solution)/shard_map/all_gather | solution.py:96
  47.5 3.2 %convolution_convert_fusion = bf16[1024,480]{0,1:T(8,128)(2,1)S(1)} fusion(bf16[1024,1280]{1,0:T(8,128)(2,1)} %all-gather.8.cloned.1.call-done, bf16[1280,480]{0,1:T(8,128)(2,1)S(1)} %copy-done), kind=kOutput, calls=%fused_computation.26 | convolution fusion | flops 1258782720 | bytes 4833280 | tf_op jit(solution)/shard_map/dot_general | solution.py:102
  55.5 23.0 %all_to_all.19 = bf16[8,128,160]{1,2,0:T(8,128)(2,1)S(1)} all-to-all(bf16[8,128,160]{1,2,0:T(8,128)(2,1)S(1)} %copy_bitcast_fusion), channel_id=1, replica_groups=mesh['ctx'=4,'vk'=4,'vg'=2] {'vk','vg'}, dimensions={0} | all-to-all | bytes 655360 | tf_op jit(solution)/shard_map/all_to_all | solution.py:104
  78.5 16.1 %all-gather.10.cloned.1.call-done = bf16[1280,1280]{1,0:T(8,128)(2,1)} async-done(((bf16[160,1280]{1,0:T(8,128)(2,1)}), bf16[1280,1280]{1,0:T(8,128)(2,1)}) %all-gather.10.cloned.1.call-update) | async-done | bytes 3276816 | tf_op jit(solution)/shard_map/all_gather | solution.py:97
  94.6 2.6 fusion.71
  98.7 47.6 %reduce-scatter.3.cloned.1.call-done = f32[1,520,256]{2,1,0:T(8,128)} async-done(((f32[8,520,256]{2,1,0:T(8,128)}), f32[1,520,256]{2,1,0:T(8,128)}) %reduce-scatter.3.cloned.1.call-update) | async-done | bytes 532496 | tf_op jit(solution)/shard_map/reduce_scatter | solution.py:61
  147.0 1.9 fusion.44
  150.7 2.0 fusion
  152.7 27.4 %all-gather.12.cloned.1.call-done = bf16[256,5120]{1,0:T(8,128)(2,1)} async-done(((bf16[32,5120]{1,0:T(8,128)(2,1)}), bf16[256,5120]{1,0:T(8,128)(2,1)}) %all-gather.12.cloned.1.call-update) | async-done | bytes 2621456 | tf_op jit(solution)/shard_map/all_gather | solution.py:109
  180.1 7.9 %multiply_reduce_fusion.4 = (f32[256]{0:T(256)S(1)}, bf16[256,1024]{1,0:T(8,128)(2,1)S(1)}) fusion(bf16[256,5120]{1,0:T(8,128)(2,1)} %all-gather.12.cloned.1.call-done, bf16[5120,1024]{1,0:T(8,128)(2,1)} %param.19), kind=kOutput, calls=%fused_computation.46 | convolution fusion | flops 2685402880 | bytes 13632512 | tf_op jit(solution)/shard_map/dot_general | solution.py:108
  193.3 15.4 %all-gather.6.cloned.1.call-done = bf16[4096,256]{1,0:T(8,128)(2,1)} async-done(((bf16[512,256]{1,0:T(8,128)(2,1)}), bf16[4096,256]{1,0:T(8,128)(2,1)}) %all-gather.6.cloned.1.call-update) | async-done | bytes 2097168 | tf_op jit(solution)/shard_map/all_gather | solution.py:67
  208.7 1.7 fusion.69
  210.4 2.0 fusion.70
  212.4 3.9 %fusion.1 = (f32[512]{0:T(512)S(1)}, bf16[512,4224]{1,0:T(8,128)(2,1)}) fusion(f32[512,4224]{1,0:T(8,128)S(1)} %get-tuple-element.14, f32[512]{0:T(512)S(1)} %get-tuple-element.13, pred[128,4224]{1,0:T(8,128)(4,1)S(1)} %pad_add_fusion), kind=kLoop, calls=%fused_computation.4 | loop fusion | flops 8650240 | bytes 13520896 | tf_op jit(solution)/shard_map/reduce_sum | solution.py:144
  216.2 27.5 %reduce-scatter.5.cloned.1.call-done = f32[1,136,256]{2,1,0:T(8,128)} async-done(((f32[8,136,256]{2,1,0:T(8,128)}), f32[1,136,256]{2,1,0:T(8,128)}) %reduce-scatter.5.cloned.1.call-update) | async-done | bytes 139280 | tf_op jit(solution)/shard_map/reduce_scatter | solution.py:61
  245.8 9.8 %all_gather.22 = bf16[1024,256]{1,0:T(8,128)(2,1)S(1)} all-gather(bf16[128,256]{1,0:T(8,128)(2,1)S(1)} %fusion.57), channel_id=1, replica_groups=mesh['ctx'=4,'vk'=4,'vg'=2] {'ctx','vg'}, dimensions={0}, use_global_device_ids=true | all-gather | bytes 589824 | tf_op jit(solution)/shard_map/all_gather | solution.py:67
  259.2 19.6 %all-gather.14.cloned.1.call-done = bf16[32,128,128]{2,1,0:T(8,128)(2,1)} async-done(((bf16[4,128,128]{2,1,0:T(8,128)(2,1)}), bf16[32,128,128]{2,1,0:T(8,128)(2,1)}) %all-gather.14.cloned.1.call-update) | async-done | bytes 1048592 | tf_op jit(solution)/shard_map/all_gather | solution.py:158
  (82 shorter events, 25.0 us)
Async XLA Ops:
  6.5 41.0 %copy-start = (bf16[1280,480]{0,1:T(8,128)(2,1)S(1)}, bf16[1280,480]{0,1:T(8,128)(2,1)}, u32[]{:S(2)}) copy-start(bf16[1280,480]{0,1:T(8,128)(2,1)} %param.16) | copy-start | bytes 3686404
  6.5 41.0 %all-gather.8.cloned.1.call-start = ((), (), s32[]{:S(2)}) async-start(), calls=%async_computation.5 | async-start | bytes 2949120 | tf_op jit(solution)/shard_map/all_gather | solution.py:96
  10.9 83.7 %all-gather.10.cloned.1.call-start = ((), (), s32[]{:S(2)}) async-start(), calls=%async_computation.6 | async-start | bytes 3686400 | tf_op jit(solution)/shard_map/all_gather | solution.py:97
  11.7 134.7 %reduce-scatter.3.cloned.1.call-start = ((), (), s32[]{:S(2)}) async-start(), calls=%async_computation.3 | async-start | bytes 4792320 | tf_op jit(solution)/shard_map/reduce_scatter | solution.py:61
  42.3 137.8 %all-gather.12.cloned.1.call-start = ((), (), s32[]{:S(2)}) async-start(), calls=%async_computation.7 | async-start | bytes 2949120 | tf_op jit(solution)/shard_map/all_gather | solution.py:109
  54.6 40.1 %copy-start.2 = (bf16[128,1280]{1,0:T(8,128)(2,1)S(1)}, bf16[128,1280]{1,0:T(8,128)(2,1)}, u32[]{:S(2)}) copy-start(bf16[128,1280]{1,0:T(8,128)(2,1)} %param.14) | copy-start | bytes 983044
  55.4 42.1 %copy-start.4 = (f32[1280]{0:T(1024)S(1)}, f32[1280]{0:T(1024)}, u32[]{:S(2)}) copy-start(f32[1280]{0:T(1024)} %param.18) | copy-start | bytes 15364
  78.5 70.5 %copy-start.5 = (s32[4,256]{1,0:T(4,128)S(1)}, s32[4,256]{1,0:T(4,128)}, u32[]{:S(2)}) copy-start(s32[4,256]{1,0:T(4,128)} %param.21) | copy-start | bytes 12292
  78.5 70.5 %copy-start.6 = (s32[4,256]{1,0:T(4,128)S(1)}, s32[4,256]{1,0:T(4,128)}, u32[]{:S(2)}) copy-start(s32[4,256]{1,0:T(4,128)} %param.20) | copy-start | bytes 12292
  98.6 110.1 %all-gather.6.cloned.1.call-start = ((), (), s32[]{:S(2)}) async-start(), calls=%async_computation.4 | async-start | bytes 2359296 | tf_op jit(solution)/shard_map/all_gather | solution.py:67
  149.0 94.8 %reduce-scatter.5.cloned.1.call-start = ((), (), s32[]{:S(2)}) async-start(), calls=%async_computation.8 | async-start | bytes 1253376 | tf_op jit(solution)/shard_map/reduce_scatter | solution.py:61
  152.7 35.3 %copy-start.8 = (f32[1024]{0:T(1024)S(1)}, f32[1024]{0:T(1024)}, u32[]{:S(2)}) copy-start(f32[1024]{0:T(1024)} %param.23) | copy-start | bytes 12292
  180.1 7.9 %copy-start.7 = (bf16[1024,1024]{1,0:T(8,128)(2,1)S(1)}, bf16[1024,1024]{1,0:T(8,128)(2,1)}, u32[]{:S(2)}) copy-start(bf16[1024,1024]{1,0:T(8,128)(2,1)} %param.24) | copy-start | bytes 6291460
  191.8 87.0 %all-gather.14.cloned.1.call-start = ((), (), s32[]{:S(2)}) async-start(), calls=%async_computation.9 | async-start | bytes 1179648 | tf_op jit(solution)/shard_map/all_gather | solution.py:158
  243.8 12.9 %copy-start.3 = (bf16[512,4224]{1,0:T(8,128)(2,1)S(1)}, bf16[512,4224]{1,0:T(8,128)(2,1)}, u32[]{:S(2)}) copy-start(bf16[512,4224]{1,0:T(8,128)(2,1)} %get-tuple-element.8) | copy-start | bytes 12976132
  256.6 25.1 %copy-start.1 = (bf16[1280,480]{0,1:T(8,128)(2,1)S(1)}, bf16[1280,480]{0,1:T(8,128)(2,1)}, u32[]{:S(2)}) copy-start(bf16[1280,480]{0,1:T(8,128)(2,1)} %param.16) | copy-start | bytes 3686404
Sparse Core Ops, SparseCore 0:
  11.0 36.4 all-gather.7
  49.1 45.4 all-gather.9
  96.9 49.3 reduce-scatter.2
  147.8 32.1 all-gather.11
  181.8 26.8 all-gather.5
  210.9 32.8 reduce-scatter.4
  259.3 19.4 all-gather.13

commit v2 on v1

--- a/solution.py
+++ b/solution.py
@@ -1,8 +1,11 @@
+import functools
 import math
 
 import jax
 import jax.numpy as jnp
 from jax import lax
+from jax.experimental import pallas as pl
+from jax.experimental.pallas import tpu as pltpu
 from jax.sharding import Mesh, PartitionSpec as P
 
 VD = 1280
@@ -16,7 +19,10 @@
 
 
 EPS = 1e-06
-VIS = ("vk", "vg")
+VIS = ("vk", "vh", "core")
+SUB = ("vh", "core")
+MESH = pl.DeviceIdType.MESH
+VMEM = pl.BlockSpec(memory_space=pltpu.VMEM)
 F32 = jnp.float32
 BF16 = jnp.bfloat16
 
@@ -38,33 +44,279 @@
         scores = jnp.einsum("qd,kd->qk", query, keys, preferred_element_type=F32) * scale
         expo = jnp.exp(scores - jnp.max(scores, axis=1, keepdims=True))
         summed = jnp.sum(expo, axis=1, keepdims=True)
-        mixed = jnp.dot(expo.astype(BF16), values, preferred_element_type=F32)
-        outs.append((mixed / summed).astype(BF16))
-    return jnp.concatenate(outs, axis=1)
-
-
-def partial_kv(rows, weight, heads, parts):
-    count = rows.shape[0]
-    raw = jnp.dot(rows, weight, preferred_element_type=F32)
+        mixed = jnp.einsum("qk,kd->dq", expo.astype(BF16), values, preferred_element_type=F32)
+        outs.append((mixed / summed.reshape(1, -1)).astype(BF16))
+    return jnp.concatenate(outs, axis=0)
+
+
+def flat_index(names, sizes):
+    index = 0
+    for name, size in zip(names, sizes):
+        index = index * size + lax.axis_index(name)
+    return index
+
+
+def coordinates(index, names, sizes):
+    place = {}
+    for name, size in reversed(list(zip(names, sizes))):
+        place[name] = index % size
+        index = index // size
+    return place
+
+
+def exchange_kernel(names, sizes, spread, count, *refs):
+    xs, outs = refs[:count], refs[count : 2 * count]
+    send_sem, recv_sem, local_sem = refs[2 * count :]
+    total = math.prod(sizes)
+    me = flat_index(names, sizes)
+    barrier = pltpu.get_barrier_semaphore()
+    for step in range(1, total):
+        pl.semaphore_signal(
+            barrier,
+            inc=1,
+            device_id=coordinates((me + step) % total, names, sizes),
+            device_id_type=MESH,
+        )
+    pl.semaphore_wait(barrier, total - 1)
+    copies = []
+    for step in range(1, total):
+        target = (me + step) % total
+        for i in range(count):
+            copy = pltpu.make_async_remote_copy(
+                src_ref=xs[i] if spread else xs[i].at[target],
+                dst_ref=outs[i].at[me],
+                send_sem=send_sem.at[i, step],
+                recv_sem=recv_sem.at[i, step],
+                device_id=coordinates(target, names, sizes),
+                device_id_type=MESH,
+            )
+            copy.start()
+            copies.append(copy)
+    for i in range(count):
+        own = pltpu.make_async_copy(
+            xs[i] if spread else xs[i].at[me], outs[i].at[me], local_sem.at[i]
+        )
+        own.start()
+        copies.append(own)
+    for copy in copies:
+        copy.wait()
+
+
+def exchange(xs, names, spread, collective_id):
+    sizes = tuple(lax.axis_size(name) for name in names)
+    total, count = math.prod(sizes), len(xs)
+    shapes = [((total,) + x.shape) if spread else x.shape for x in xs]
+    return pl.pallas_call(
+        functools.partial(exchange_kernel, names, sizes, spread, count),
+        out_shape=[jax.ShapeDtypeStruct(sh, x.dtype) for sh, x in zip(shapes, xs)],
+        in_specs=[VMEM] * count,
+        out_specs=[VMEM] * count,
+        scratch_shapes=[
+            pltpu.SemaphoreType.DMA((count, total)),
+            pltpu.SemaphoreType.DMA((count, total)),
+            pltpu.SemaphoreType.DMA((count,)),
+        ],
+        compiler_params=pltpu.CompilerParams(
+            collective_id=collective_id, has_side_effects=True
+        ),
+        cost_estimate=pl.CostEstimate(flops=0, bytes_accessed=30_000_000, transcendentals=0),
+    )(*xs)
+
+
+def line_kernel(sizes, chunks, x_ref, out_ref, send_sem, recv_sem, share_send, share_recv, local_sem):
+    chips = sizes[0] * sizes[1]
+    core = lax.axis_index("core")
+    chip = lax.axis_index("vk") * sizes[1] + lax.axis_index("vh")
+    rows = x_ref.shape[0] // chunks
+
+    def at(where, which):
+        return {"vk": where // sizes[1], "vh": where % sizes[1], "core": which}
+
+    def neighbour(direction):
+        return chip + 1 if direction == 0 else chip - 1
+
+    def has(direction):
+        return chip < chips - 1 if direction == 0 else chip > 0
+
+    barrier = pltpu.get_barrier_semaphore()
+    pl.semaphore_signal(barrier, inc=1, device_id=at(chip, 1 - core), device_id_type=MESH)
+    for direction in range(2):
+        @pl.when(has(direction))
+        def _():
+            pl.semaphore_signal(
+                barrier, inc=1, device_id=at(neighbour(direction), core), device_id_type=MESH
+            )
+    pl.semaphore_wait(barrier, 1 + jnp.where(has(0), 1, 0) + jnp.where(has(1), 1, 0))
+
+    def slot(origin, which, piece):
+        return out_ref.at[origin * 2 + which, pl.ds(piece * rows, rows)]
+
+    def source(origin, piece, hop):
+        return x_ref.at[pl.ds(piece * rows, rows)] if hop == 0 else slot(origin, core, piece)
+
+    def origin_of(direction, hop):
+        return chip - hop if direction == 0 else chip + hop
+
+    def exists(direction, hop):
+        return chip >= hop if direction == 0 else chip + hop < chips
+
+    def pass_on(direction, hop, piece):
+        origin = origin_of(direction, hop)
+        return pltpu.make_async_remote_copy(
+            src_ref=source(origin, piece, hop),
+            dst_ref=slot(origin, core, piece),
+            send_sem=send_sem.at[direction, hop, piece],
+            recv_sem=recv_sem.at[direction, hop, piece],
+            device_id=at(neighbour(direction), core),
+            device_id_type=MESH,
+        )
+
+    def arrival(direction, hop, piece):
+        origin = origin_of(direction, hop)
+        return pltpu.make_async_remote_copy(
+            src_ref=slot(origin, core, piece),
+            dst_ref=slot(origin, core, piece),
+            send_sem=send_sem.at[direction, hop - 1, piece],
+            recv_sem=recv_sem.at[direction, hop - 1, piece],
+            device_id=at(chip, 1 - core),
+            device_id_type=MESH,
+        )
+
+    def share(origin, piece, hop):
+        return pltpu.make_async_remote_copy(
+            src_ref=source(origin, piece, hop),
+            dst_ref=slot(origin, core, piece),
+            send_sem=share_send.at[origin, piece],
+            recv_sem=share_recv.at[origin, piece],
+            device_id=at(chip, 1 - core),
+            device_id_type=MESH,
+        )
+
+    for piece in range(chunks):
+        for direction in range(2):
+            @pl.when(has(direction))
+            def _():
+                pass_on(direction, 0, piece).start()
+    own = pltpu.make_async_copy(x_ref, out_ref.at[chip * 2 + core], local_sem)
+    own.start()
+    for piece in range(chunks):
+        share(chip, piece, 0).start()
+    for hop in range(1, chips):
+        for piece in range(chunks):
+            for direction in range(2):
+                @pl.when(exists(direction, hop))
+                def _():
+                    arrival(direction, hop, piece).wait_recv()
+                    if hop < chips - 1:
+                        @pl.when(has(direction))
+                        def _():
+                            pass_on(direction, hop, piece).start()
+                    share(origin_of(direction, hop), piece, hop).start()
+    own.wait()
+    for piece in range(chunks):
+        share(chip, piece, 0).wait_send()
+        for direction in range(2):
+            for hop in range(chips):
+                if hop < chips - 1:
+                    @pl.when(jnp.logical_and(exists(direction, hop), has(direction)))
+                    def _():
+                        pass_on(direction, hop, piece).wait_send()
+                if hop > 0:
+                    @pl.when(exists(direction, hop))
+                    def _():
+                        share(origin_of(direction, hop), piece, hop).wait_send()
+        for origin in range(chips):
+            pltpu.make_async_remote_copy(
+                src_ref=slot(origin, 1 - core, piece),
+                dst_ref=slot(origin, 1 - core, piece),
+                send_sem=share_send.at[origin, piece],
+                recv_sem=share_recv.at[origin, piece],
+                device_id=at(chip, 1 - core),
+                device_id_type=MESH,
+            ).wait_recv()
+
+
+def line_gather(x, chunks, collective_id):
+    sizes = tuple(lax.axis_size(name) for name in VIS)
+    chips = sizes[0] * sizes[1]
+    return pl.pallas_call(
+        functools.partial(line_kernel, sizes, chunks),
+        out_shape=jax.ShapeDtypeStruct((2 * chips,) + x.shape, x.dtype),
+        in_specs=[VMEM],
+        out_specs=VMEM,
+        scratch_shapes=[
+            pltpu.SemaphoreType.DMA((2, chips, chunks)),
+            pltpu.SemaphoreType.DMA((2, chips, chunks)),
+            pltpu.SemaphoreType.DMA((chips, chunks)),
+            pltpu.SemaphoreType.DMA((chips, chunks)),
+            pltpu.SemaphoreType.DMA,
+        ],
+        compiler_params=pltpu.CompilerParams(
+            collective_id=collective_id, has_side_effects=True
+        ),
+        cost_estimate=pl.CostEstimate(flops=0, bytes_accessed=70_000_000, transcendentals=0),
+    )(x)
+
+
+def text_kernel(rows_ref, weight_ref, out_ref):
+    rows = rows_ref[...]
+    each = rows.shape[0]
+    out_ref[0, :each, :] = jnp.dot(rows, weight_ref[0], preferred_element_type=F32)
     floats = rows.astype(F32)
-    squares = jnp.sum(floats * floats, axis=1)
+    squares = floats * floats
+    coarse = squares.astype(BF16)
+    rest = (squares - coarse.astype(F32)).astype(BF16)
+    ones = jnp.ones((8, rows.shape[1]), BF16)
+    dims = (((1,), (1,)), ((), ()))
+    sums = lax.dot_general(ones, coarse, dims, preferred_element_type=F32)
+    sums += lax.dot_general(ones, rest, dims, preferred_element_type=F32)
+    out_ref[0, each:, :] = sums[:, : 2 * HD]
+    for part in range(1, each // (2 * HD)):
+        out_ref[0, each + part : each + part + 1, :] = sums[:1, part * 2 * HD : (part + 1) * 2 * HD]
+
+
+def text_partial(text, weight, parts):
+    count, depth = text.shape
     each = count // parts
-    pieces = raw.reshape(parts, each, 2, heads, HD).transpose(3, 0, 1, 2, 4)
-    pieces = pieces.reshape(heads * parts, each, 2 * HD)
-    extra = squares.reshape(parts, each // HD // 2 if each >= 2 * HD else 1, -1)
-    extra = jnp.pad(extra, ((0, 0), (0, 8 - extra.shape[1]), (0, 2 * HD - extra.shape[2])))
-    extra = jnp.broadcast_to(extra[None], (heads,) + extra.shape).reshape(heads * parts, 8, 2 * HD)
-    return jnp.concatenate([pieces, extra], axis=1)
-
-
-def whole_kv(partial, count):
+    return pl.pallas_call(
+        text_kernel,
+        grid=(parts, KVH),
+        out_shape=jax.ShapeDtypeStruct((KVH * parts, each + 8, 2 * HD), F32),
+        in_specs=[
+            pl.BlockSpec((each, depth), lambda p, h: (p, 0)),
+            pl.BlockSpec((1, depth, 2 * HD), lambda p, h: (h, 0, 0)),
+        ],
+        out_specs=pl.BlockSpec((1, each + 8, 2 * HD), lambda p, h: (h * parts + p, 0, 0)),
+        cost_estimate=pl.CostEstimate(
+            flops=2 * count * depth * KVH * 2 * HD,
+            bytes_accessed=10_000_000,
+            transcendentals=0,
+        ),
+    )(text, weight)
+
+
+def whole_text(partial):
     total = lax.psum_scatter(partial, VIS, scatter_dimension=0, tiled=True)[0]
     each = total.shape[0] - 8
-    rows = each // HD // 2 if each >= 2 * HD else 1
-    squares = total[each : each + rows, : each // rows].reshape(each)
+    squares = total[each : each + each // (2 * HD)].reshape(each)
     inverse = lax.rsqrt(squares / D + EPS)
     share = (total[:each] * inverse[:, None]).astype(BF16)
-    return lax.all_gather(share, ("ctx", "vg"), axis=0, tiled=True)
+    return lax.all_gather(share, ("ctx",) + SUB, axis=0, tiled=True)
+
+
+def whole_image(visual, weight, parts):
+    each = visual.shape[0] // parts
+    raw = jnp.einsum("rd,hde->hre", visual, weight, preferred_element_type=F32)
+    pieces = raw.astype(BF16).reshape(KVH * parts, each, 2 * HD)
+    floats = visual.astype(F32)
+    squares = jnp.sum(floats * floats, axis=1).reshape(1, parts, 1, each)
+    squares = jnp.broadcast_to(squares, (KVH, parts, 8, each)).reshape(KVH * parts, 8, each)
+    pieces, squares = exchange((pieces, squares), VIS, False, 3)
+    total = jnp.sum(pieces.astype(F32), axis=0)
+    inverse = lax.rsqrt(jnp.sum(squares[:, 0, :], axis=0) / D + EPS)
+    share = (total * inverse[:, None]).astype(BF16)
+    (whole,) = exchange((share,), ("ctx",) + SUB, True, 4)
+    return whole.reshape(-1, 2 * HD)
 
 
 def per_device(
@@ -83,32 +335,36 @@
     resp_kv,
     resp_len,
 ):
-    vis_count = lax.axis_size("vk") * lax.axis_size("vg")
-    parts = lax.axis_size("vg")
+    parts = lax.axis_size("vh") * lax.axis_size("core")
+    vis_count = lax.axis_size("vk") * parts
     ctx_count = lax.axis_size("ctx")
-    vis_index = lax.axis_index("vk") * parts + lax.axis_index("vg")
+    vis_index = flat_index(VIS, tuple(lax.axis_size(name) for name in VIS))
     patch_count = patches.shape[0]
     shard_rows = prompt_text.shape[0]
     local_heads = VHEADS // vis_count
 
     floats = patches.astype(F32)
     normed = layer_norm(floats, vis_gain).astype(BF16)
-    gathered = lax.all_gather(normed, VIS, axis=0, tiled=True)
+    gathered = line_gather(normed, 2, 0).reshape(-1, VD)
     w_out_all = lax.all_gather(w_out, VIS, axis=0, tiled=True)
 
     weight = (w_kv.astype(F32) * kv_gain[:, None]).astype(BF16)
-    text_kv = whole_kv(partial_kv(prompt_text, weight, KVH, parts), shard_rows)
+    weight = weight.reshape(-1, 2, KVH, HD).transpose(2, 0, 1, 3).reshape(KVH, -1, 2 * HD)
+    text_kv = whole_text(text_partial(prompt_text, weight, parts))
 
     qkv = jnp.dot(gathered, w_qkv, preferred_element_type=F32).astype(BF16)
     heads = vision_attention(qkv, local_heads)
-    returned = lax.all_to_all(heads, VIS, split_axis=0, concat_axis=1, tiled=True)
-    projected = jnp.dot(returned, w_out_all, preferred_element_type=F32)
+    heads = heads.reshape(-1, vis_count, patch_count).transpose(1, 0, 2)
+    (returned,) = exchange((heads,), VIS, False, 1)
+    projected = jnp.einsum(
+        "dp,de->pe", returned.reshape(VD, patch_count), w_out_all, preferred_element_type=F32
+    )
     mixed = floats + projected
     merged = layer_norm(mixed, merge_gain).astype(BF16).reshape(patch_count // 4, MD)
     visual = jnp.dot(
-        lax.all_gather(merged, VIS, axis=0, tiled=True), w_merge, preferred_element_type=F32
+        line_gather(merged, 2, 2).reshape(-1, MD), w_merge, preferred_element_type=F32
     ).astype(BF16)
-    image_kv = whole_kv(partial_kv(visual, weight, KVH, parts), visual.shape[0])
+    image_kv = whole_image(visual, weight, parts)
 
     flat = (token_dest * shard_rows + token_row).reshape(-1)
     positions = jnp.arange(ctx_count * shard_rows, dtype=jnp.int32)
@@ -154,15 +410,16 @@
     )
     live = jnp.tile(query_positions < resp_len[0], mine)[:, None]
     result = jnp.where(live, mix / summed, 0.0).astype(BF16)
-    result = result.reshape(mine, resp_rows, HD)
-    whole = lax.all_gather(result, VIS, axis=0, tiled=True)
+    result = result.reshape(mine, resp_rows, HD).transpose(1, 0, 2)
+    whole = line_gather(result.reshape(resp_rows, mine * HD), 2, 5)
     return whole.transpose(1, 0, 2).reshape(resp_rows, QH * HD)
 
 
 def solution(mesh):
     ctx_count, vis_count = mesh.shape["ctx"], mesh.shape["vis"]
-    parts = max(1, vis_count // KVH)
-    fine = Mesh(mesh.devices.reshape(ctx_count, vis_count // parts, parts), ("ctx", "vk", "vg"))
+    parts = vis_count // KVH
+    shape = (ctx_count, vis_count // parts, parts // 2, 2)
+    fine = Mesh(mesh.devices.reshape(shape), ("ctx",) + VIS)
     return jax.shard_map(
         per_device,
         mesh=fine,

time: 289 us -> 251 us (0.87)
  Pallas kernels: 0 us -> 149 us
  waiting for transfers between devices: 160 us -> 29.4 us
  blocking collectives: 32.8 us -> 0 us
  local copies, waits for them, and re-layouts: 26.4 us -> 17.5 us
  other arithmetic: 25.2 us -> 16.5 us
  matrix products: 29.6 us -> 23.9 us
    pallas_call x0 -> x7, Pallas kernels: none -> 149 us  [the longest x3 102 us: line_gather(): pl.pallas_call(functools.partial(line_kernel, sizes, chunks), out_shape=j...]
    reduce_scatter x2 -> x1, waiting for transfers between devices: 75.2 us -> 0.02 us  [whole_text(): total = lax.psum_scatter(partial, VIS, scatter_dimension=0, tiled=True)[0]]
    all_gather x4 -> x1, waiting for transfers between devices: 67.5 us -> 0.02 us  [whole_text(): return lax.all_gather(share, ('ctx',) + SUB, axis=0, tiled=True)]
    all_to_all x1 -> x0, blocking collectives: 23 us -> none  [per_device(): lax.all_to_all(heads, VIS, split_axis=0, concat_axis=1, tiled=True)]
    all_gather x1, waiting for transfers between devices: 16.1 us -> 28.6 us  [per_device(): w_out_all = lax.all_gather(w_out, VIS, axis=0, tiled=True)]
    all_gather x1 -> x0, blocking collectives: 9.78 us -> none  [whole_kv(): return lax.all_gather(share, ('ctx', 'vg'), axis=0, tiled=True)]
    reshape x6 -> x4, local copies, waits for them, and re-layouts: 18.3 us -> 8.68 us  [the longest x3 8.58 us: per_device(): weight.reshape(-1, 2, KVH, HD).transpose(2, 0, 1, 3)]
    dot_general x6 -> x5, matrix products: 19.9 us -> 13.8 us  [the longest x1 7.86 us: per_device(): jnp.dot(line_gather(merged, 2, 2).reshape(-1, MD), w_merge, preferred_ele...]
  transfers between devices with their start and end apart: 7 -> 3, of which waited for: 7 -> 1; matrix products, arithmetic and copies ran while one was open for 24% -> 14% of each run, Pallas kernels for 0% -> 48%
where the time goes in v2:
time: 251 us; the launch traced here: 250 us
  Pallas kernels  149 us (59%)
  waiting for transfers between devices  29.4 us (12%)
  matrix products  23.9 us (10%)
  local copies, waits for them, and re-layouts  17.5 us (7%)
  other arithmetic  16.5 us (7%)
  between operations  14.1 us (6%)
    pallas_call x3, Pallas kernels, line_gather(): pl.pallas_call(functools.partial(line_kernel, sizes, chunks), out_shape=j...  102 us
    pallas_call x3, Pallas kernels, exchange(): pl.pallas_call(functools.partial(exchange_kernel, names, sizes, spread, c...  36.3 us
    all_gather x1, waiting for transfers between devices, per_device(): w_out_all = lax.all_gather(w_out, VIS, axis=0, tiled=True)  28.6 us
    pallas_call x1, Pallas kernels, text_partial(): pl.pallas_call(text_kernel, grid=(parts, KVH), out_shape=jax.ShapeDtypeSt...  10.9 us
    reshape x3, local copies, waits for them, and re-layouts, per_device(): weight.reshape(-1, 2, KVH, HD).transpose(2, 0, 1, 3)  8.58 us
    dot_general x1, matrix products, per_device(): jnp.dot(line_gather(merged, 2, 2).reshape(-1, MD), w_merge, preferred_ele...  7.86 us
  transfers between devices with their start and end apart: 3, of which 1 were waited for; matrix products, arithmetic and copies ran while one was open for 14% of the time, Pallas kernels for 48%

profile of v2, /device:TPU:0, one launch (start us, length us, event | category | flops | bytes accessed | tf_op | source)
XLA Modules:
  0.0 250.4 jit_solution(12856047109665026814)
XLA Ops:
  6.5 2.1 multiply_convert_fusion
  8.6 2.7 %reshape.142 = bf16[1024,2,4,128]{3,2,1,0:T(4,128)(2,1)} reshape(bf16[1024,1024]{1,0:T(8,128)(2,1)S(1)} %multiply_convert_fusion) | data formatting | bytes 4194304 | tf_op jit(solution)/shard_map/reshape | solution.py:352
  11.4 3.2 %copy.44 = bf16[1024,2,4,128]{3,1,0,2:T(2,128)(2,1)S(1)} copy(bf16[1024,2,4,128]{3,2,1,0:T(4,128)(2,1)} %reshape.142) | data formatting | bytes 4194304 | tf_op jit(solution)/shard_map/reshape | solution.py:352
  14.6 2.6 %reshape.143.weight_ref = bf16[4,1024,256]{2,1,0:T(8,128)(2,1)} reshape(bf16[4,1024,2,128]{3,2,1,0:T(2,128)(2,1)S(1)} %bitcast.67) | data formatting | bytes 4194304 | tf_op jit(solution)/shard_map/reshape | solution.py:352
  17.2 10.9 %shard_map.136 = f32[8,520,256]{2,1,0:T(8,128)} custom-call(bf16[1024,1024]{1,0:T(8,128)(2,1)} %rows_ref.1, bf16[4,1024,256]{2,1,0:T(8,128)(2,1)} %reshape.143.weight_ref), custom_call_target="tpu_custom_call" | custom-call | flops 2147483648 | bytes 10000000 | tf_op jit(solution)/shard_map/pallas_call | solution.py:281
  30.3 2.0 fusion
  33.6 56.1 %shard_map.137 = bf16[8,128,1280]{2,1,0:T(8,128)(2,1)} custom-call(bf16[128,1280]{1,0:T(8,128)(2,1)} %fusion.41.x_ref), custom_call_target="tpu_custom_call" | custom-call | bytes 70000000 | tf_op jit(solution)/shard_map/pallas_call | solution.py:242
  89.7 3.3 %convolution_convert_fusion = bf16[1024,480]{0,1:T(8,128)(2,1)S(1)} fusion(bf16[1024,1280]{1,0:T(8,128)(2,1)} %bitcast.71, bf16[1280,480]{0,1:T(8,128)(2,1)S(1)} %copy-done), kind=kOutput, calls=%fused_computation.24 | convolution fusion | flops 1258782720 | bytes 4833280 | tf_op jit(solution)/shard_map/dot_general | solution.py:355
  98.5 10.7 %shard_map.138 = bf16[8,160,128]{2,1,0:T(8,128)(2,1)} custom-call(bf16[8,160,128]{2,1,0:T(8,128)(2,1)} %bitcast_bitcast_fusion.refs_0_), custom_call_target="tpu_custom_call" | custom-call | bytes 30000000 | tf_op jit(solution)/shard_map/pallas_call | solution.py:109
  111.6 1.9 fusion.43
  113.5 28.6 %all-gather.5.cloned.1.call-done = bf16[1280,1280]{1,0:T(8,128)(2,1)} async-done(((bf16[160,1280]{1,0:T(8,128)(2,1)}), bf16[1280,1280]{1,0:T(8,128)(2,1)}) %all-gather.5.cloned.1.call-update) | async-done | bytes 3276816 | tf_op jit(solution)/shard_map/all_gather | solution.py:349
  142.1 2.8 %fusion.66 = (f32[128]{0:T(128)S(1)}, f32[128,1280]{1,0:T(8,128)S(1)}) fusion(bf16[1280,128]{1,0:T(8,128)(2,1)} %bitcast.72, bf16[1280,1280]{1,0:T(8,128)(2,1)} %all-gather.5.cloned.1.call-done, bf16[128,1280]{1,0:T(8,128)(2,1)S(1)} %copy-done.3), kind=kOutput, calls=%fused_computation.100 | convolution fusion | flops 419921792 | bytes 4588032 | tf_op jit(solution)/shard_map/dp,de->pe/dot_general | solution.py:359
  146.2 27.8 %shard_map.139 = bf16[8,32,5120]{2,1,0:T(8,128)(2,1)} custom-call(bf16[32,5120]{1,0:T(8,128)(2,1)} %reshape.147.x_ref), custom_call_target="tpu_custom_call" | custom-call | bytes 70000000 | tf_op jit(solution)/shard_map/pallas_call | solution.py:242
  174.1 7.9 %multiply_reduce_fusion.3 = (f32[256]{0:T(256)S(1)}, bf16[256,1024]{1,0:T(8,128)(2,1)S(1)}) fusion(bf16[256,5120]{1,0:T(8,128)(2,1)} %bitcast.70, bf16[5120,1024]{1,0:T(8,128)(2,1)} %param.19), kind=kOutput, calls=%fused_computation.45 | convolution fusion | flops 2685402880 | bytes 13632512 | tf_op jit(solution)/shard_map/dot_general | solution.py:364
  182.0 1.5 convolution_convert_fusion.2
  184.1 14.1 %shard_map.140 = (bf16[8,128,256]{2,1,0:T(8,128)(2,1)}, f32[8,8,128]{2,1,0:T(8,128)}) custom-call(bf16[8,128,256]{2,1,0:T(8,128)(2,1)} %bitcast.78, f32[8,8,128]{2,1,0:T(8,128)} %broadcast_in_dim.71.refs_1_), custom_call_target="tpu_custom_call" | custom-call | bytes 30000000 | tf_op jit(solution)/shard_map/pallas_call | solution.py:109
  200.9 11.4 %shard_map.141 = bf16[8,128,256]{2,1,0:T(8,128)(2,1)} custom-call(bf16[128,256]{1,0:T(8,128)(2,1)} %multiply_convert_fusion.2.refs_0_), custom_call_target="tpu_custom_call" | custom-call | bytes 30000000 | tf_op jit(solution)/shard_map/pallas_call | solution.py:109
  212.3 1.5 multiply_reduce_fusion.2
  213.8 1.7 fusion.64
  215.5 2.0 fusion.65
  217.5 2.6 %fusion.1 = (f32[512]{0:T(512)S(1)}, bf16[512,4224]{1,0:T(8,128)(2,1)S(1)}) fusion(f32[512,4224]{1,0:T(8,128)S(1)} %get-tuple-element.18, f32[512]{0:T(512)S(1)} %get-tuple-element.17, pred[128,4224]{1,0:T(8,128)(4,1)S(1)} %pad_add_fusion), kind=kLoop, calls=%fused_computation.4 | loop fusion | flops 8650240 | bytes 13520896 | tf_op jit(solution)/shard_map/reduce_sum | solution.py:400
  223.3 17.6 %shard_map.142 = bf16[8,128,512]{2,1,0:T(8,128)(2,1)} custom-call(bf16[128,512]{1,0:T(8,128)(2,1)} %bitcast.77), custom_call_target="tpu_custom_call" | custom-call | bytes 70000000 | tf_op jit(solution)/shard_map/pallas_call | solution.py:242
  240.9 1.6 copy.34
  242.5 1.3 copy.35
  (70 shorter events, 18.3 us)
Async XLA Ops:
  6.5 83.2 %copy-start = (bf16[1280,480]{0,1:T(8,128)(2,1)S(1)}, bf16[1280,480]{0,1:T(8,128)(2,1)}, u32[]{:S(2)}) copy-start(bf16[1280,480]{0,1:T(8,128)(2,1)} %param.16) | copy-start | bytes 3686404
  6.5 104.3 %reduce-scatter.2.cloned.1.call-start = ((), (), s32[]{:S(2)}) async-start(), calls=%async_computation.1 | async-start | bytes 4792320 | tf_op jit(solution)/shard_map/reduce_scatter | solution.py:299
  28.2 2.1 copy-start.7
  28.2 2.1 copy-start.8
  28.2 4.1 %copy-start.3 = (bf16[128,1280]{1,0:T(8,128)(2,1)S(1)}, bf16[128,1280]{1,0:T(8,128)(2,1)}, u32[]{:S(2)}) copy-start(bf16[128,1280]{1,0:T(8,128)(2,1)} %param.14) | copy-start | bytes 983044
  28.2 4.5 %copy-start.6 = (f32[1280]{0:T(1024)S(1)}, f32[1280]{0:T(1024)}, u32[]{:S(2)}) copy-start(f32[1280]{0:T(1024)} %param.15) | copy-start | bytes 15364
  28.2 113.9 %all-gather.5.cloned.1.call-start = ((), (), s32[]{:S(2)}) async-start(), calls=%async_computation.3 | async-start | bytes 3686400 | tf_op jit(solution)/shard_map/all_gather | solution.py:349
  29.0 184.9 %all-gather.3.cloned.1.call-start = ((), (), s32[]{:S(2)}) async-start(), calls=%async_computation.2 | async-start | bytes 2359296 | tf_op jit(solution)/shard_map/all_gather | solution.py:304
  110.8 34.3 %copy-start.5 = (f32[1280]{0:T(1024)S(1)}, f32[1280]{0:T(1024)}, u32[]{:S(2)}) copy-start(f32[1280]{0:T(1024)} %param.18) | copy-start | bytes 15364
  174.1 7.9 %copy-start.2 = (bf16[4,1024,256]{2,1,0:T(8,128)(2,1)S(1)}, bf16[4,1024,256]{2,1,0:T(8,128)(2,1)}, u32[]{:S(2)}) copy-start(bf16[4,1024,256]{2,1,0:T(8,128)(2,1)} %reshape.143.weight_ref) | copy-start | bytes 6291460
  220.6 1.3 copy-start.4
  221.9 21.9 %copy-start.1 = (bf16[1280,480]{0,1:T(8,128)(2,1)S(1)}, bf16[1280,480]{0,1:T(8,128)(2,1)}, u32[]{:S(2)}) copy-start(bf16[1280,480]{0,1:T(8,128)(2,1)} %param.16) | copy-start | bytes 3686404
Sparse Core Ops, SparseCore 0:
  28.3 71.2 reduce-scatter.1
  101.3 40.8 all-gather.4
  144.0 26.6 all-gather.2

commit v3 on v2

--- a/solution.py
+++ b/solution.py
@@ -258,45 +258,70 @@
     )(x)
 
 
-def text_kernel(rows_ref, weight_ref, out_ref):
+def project_kernel(joined, rows_ref, key_ref, value_ref, out_ref, *rest):
+    sums_ref = rest[-1]
+    each = rows_ref.shape[0]
     rows = rows_ref[...]
-    each = rows.shape[0]
-    out_ref[0, :each, :] = jnp.dot(rows, weight_ref[0], preferred_element_type=F32)
-    floats = rows.astype(F32)
-    squares = floats * floats
-    coarse = squares.astype(BF16)
-    rest = (squares - coarse.astype(F32)).astype(BF16)
-    ones = jnp.ones((8, rows.shape[1]), BF16)
-    dims = (((1,), (1,)), ((), ()))
-    sums = lax.dot_general(ones, coarse, dims, preferred_element_type=F32)
-    sums += lax.dot_general(ones, rest, dims, preferred_element_type=F32)
-    out_ref[0, each:, :] = sums[:, : 2 * HD]
-    for part in range(1, each // (2 * HD)):
-        out_ref[0, each + part : each + part + 1, :] = sums[:1, part * 2 * HD : (part + 1) * 2 * HD]
-
-
-def text_partial(text, weight, parts):
-    count, depth = text.shape
+
+    @pl.when(pl.program_id(1) == 0)
+    def _():
+        floats = rows.astype(F32)
+        squares = floats * floats
+        coarse = squares.astype(BF16)
+        fine = (squares - coarse.astype(F32)).astype(BF16)
+        ones = jnp.ones((8, rows.shape[1]), BF16)
+        dims = (((1,), (1,)), ((), ()))
+        sums_ref[...] = lax.dot_general(
+            ones, coarse, dims, preferred_element_type=F32
+        ) + lax.dot_general(ones, fine, dims, preferred_element_type=F32)
+
+    both = jnp.concatenate([key_ref[...], value_ref[...]], axis=1)
+    raw = jnp.dot(rows, both, preferred_element_type=F32)
+    if joined:
+        out_ref[0, :each, :] = raw
+        out_ref[0, each:, :] = sums_ref[:, : 2 * HD]
+        for part in range(1, each // (2 * HD)):
+            out_ref[0, each + part : each + part + 1, :] = sums_ref[
+                :1, part * 2 * HD : (part + 1) * 2 * HD
+            ]
+    else:
+        out_ref[0] = raw.astype(BF16)
+        rest[0][0] = sums_ref[...]
+
+
+def project(rows, weight, parts, joined):
+    count, depth = rows.shape
     each = count // parts
+    pieces = KVH * parts
+    place = lambda p, h: (h * parts + p, 0, 0)
+    if joined:
+        shapes = [jax.ShapeDtypeStruct((pieces, each + 8, 2 * HD), F32)]
+    else:
+        shapes = [
+            jax.ShapeDtypeStruct((pieces, each, 2 * HD), BF16),
+            jax.ShapeDtypeStruct((pieces, 8, each), F32),
+        ]
     return pl.pallas_call(
-        text_kernel,
+        functools.partial(project_kernel, joined),
         grid=(parts, KVH),
-        out_shape=jax.ShapeDtypeStruct((KVH * parts, each + 8, 2 * HD), F32),
+        out_shape=shapes,
         in_specs=[
             pl.BlockSpec((each, depth), lambda p, h: (p, 0)),
-            pl.BlockSpec((1, depth, 2 * HD), lambda p, h: (h, 0, 0)),
+            pl.BlockSpec((depth, HD), lambda p, h: (0, h)),
+            pl.BlockSpec((depth, HD), lambda p, h: (0, KVH + h)),
         ],
-        out_specs=pl.BlockSpec((1, each + 8, 2 * HD), lambda p, h: (h * parts + p, 0, 0)),
+        out_specs=[pl.BlockSpec((1,) + shape.shape[1:], place) for shape in shapes],
+        scratch_shapes=[pltpu.VMEM((8, each), F32)],
         cost_estimate=pl.CostEstimate(
             flops=2 * count * depth * KVH * 2 * HD,
-            bytes_accessed=10_000_000,
+            bytes_accessed=count * depth * 10,
             transcendentals=0,
         ),
-    )(text, weight)
-
-
-def whole_text(partial):
-    total = lax.psum_scatter(partial, VIS, scatter_dimension=0, tiled=True)[0]
+    )(rows, weight, weight)
+
+
+def whole_text(total):
+    total = total[0]
     each = total.shape[0] - 8
     squares = total[each : each + each // (2 * HD)].reshape(each)
     inverse = lax.rsqrt(squares / D + EPS)
@@ -305,12 +330,7 @@
 
 
 def whole_image(visual, weight, parts):
-    each = visual.shape[0] // parts
-    raw = jnp.einsum("rd,hde->hre", visual, weight, preferred_element_type=F32)
-    pieces = raw.astype(BF16).reshape(KVH * parts, each, 2 * HD)
-    floats = visual.astype(F32)
-    squares = jnp.sum(floats * floats, axis=1).reshape(1, parts, 1, each)
-    squares = jnp.broadcast_to(squares, (KVH, parts, 8, each)).reshape(KVH * parts, 8, each)
+    pieces, squares = project(visual, weight, parts, False)
     pieces, squares = exchange((pieces, squares), VIS, False, 3)
     total = jnp.sum(pieces.astype(F32), axis=0)
     inverse = lax.rsqrt(jnp.sum(squares[:, 0, :], axis=0) / D + EPS)
@@ -349,8 +369,10 @@
     w_out_all = lax.all_gather(w_out, VIS, axis=0, tiled=True)
 
     weight = (w_kv.astype(F32) * kv_gain[:, None]).astype(BF16)
-    weight = weight.reshape(-1, 2, KVH, HD).transpose(2, 0, 1, 3).reshape(KVH, -1, 2 * HD)
-    text_kv = whole_text(text_partial(prompt_text, weight, parts))
+    weight, gathered, w_out_all = lax.optimization_barrier((weight, gathered, w_out_all))
+    text_total = lax.psum_scatter(
+        project(prompt_text, weight, parts, True)[0], VIS, scatter_dimension=0, tiled=True
+    )
 
     qkv = jnp.dot(gathered, w_qkv, preferred_element_type=F32).astype(BF16)
     heads = vision_attention(qkv, local_heads)
@@ -361,9 +383,10 @@
     )
     mixed = floats + projected
     merged = layer_norm(mixed, merge_gain).astype(BF16).reshape(patch_count // 4, MD)
-    visual = jnp.dot(
-        line_gather(merged, 2, 2).reshape(-1, MD), w_merge, preferred_element_type=F32
-    ).astype(BF16)
+    merged = line_gather(merged, 2, 2).reshape(-1, MD)
+    merged, text_total = lax.optimization_barrier((merged, text_total))
+    text_kv = whole_text(text_total)
+    visual = jnp.dot(merged, w_merge, preferred_element_type=F32).astype(BF16)
     image_kv = whole_image(visual, weight, parts)
 
     flat = (token_dest * shard_rows + token_row).reshape(-1)

time: 251 us -> 245 us (0.976)
  Pallas kernels: 149 us -> 179 us
  waiting for transfers between devices: 29.4 us -> 0.78 us
  local copies, waits for them, and re-layouts: 17.5 us -> 8.35 us
  other arithmetic: 16.5 us -> 19.1 us
    all_gather x1, waiting for transfers between devices: 28.6 us -> 0.01 us  [per_device(): w_out_all = lax.all_gather(w_out, VIS, axis=0, tiled=True)]
    pallas_call x3, Pallas kernels: 102 us -> 120 us  [line_gather(): pl.pallas_call(functools.partial(line_kernel, sizes, chunks), out_shape=j...]
    reshape x3 -> x0, local copies, waits for them, and re-layouts: 8.58 us -> none  [per_device(): weight.reshape(-1, 2, KVH, HD).transpose(2, 0, 1, 3)]
    pallas_call x1 -> x2, Pallas kernels: 10.9 us -> 17.8 us  [project(): pl.pallas_call(functools.partial(project_kernel, joined), grid=(parts, KV...]
    pallas_call x3, Pallas kernels: 36.3 us -> 41.3 us  [exchange(): pl.pallas_call(functools.partial(exchange_kernel, names, sizes, spread, c...]
    dot_general x2 -> x1, matrix products: 9.38 us -> 8.44 us  [per_device(): visual = jnp.dot(merged, w_merge, preferred_element_type=F32).astype(BF16)]
  transfers between devices with their start and end apart: 3 -> 3, of which waited for: 1 -> 0; matrix products, arithmetic and copies ran while one was open for 14% -> 14% of each run, Pallas kernels for 48% -> 62%
where the time goes in v3:
time: 245 us; the launch traced here: 244 us
  Pallas kernels  179 us (73%)
  matrix products  22.9 us (9%)
  other arithmetic  19.1 us (8%)
  between operations  14.1 us (6%)
  local copies, waits for them, and re-layouts  8.35 us (3%)
    pallas_call x3, Pallas kernels, line_gather(): pl.pallas_call(functools.partial(line_kernel, sizes, chunks), out_shape=j...  120 us
    pallas_call x3, Pallas kernels, exchange(): pl.pallas_call(functools.partial(exchange_kernel, names, sizes, spread, c...  41.3 us
    pallas_call x2, Pallas kernels, project(): pl.pallas_call(functools.partial(project_kernel, joined), grid=(parts, KV...  17.8 us
    dot_general x1, matrix products, per_device(): visual = jnp.dot(merged, w_merge, preferred_element_type=F32).astype(BF16)  8.44 us
  transfers between devices with their start and end apart: 3, of which 0 were waited for; matrix products, arithmetic and copies ran while one was open for 14% of the time, Pallas kernels for 62%

profile of v3, /device:TPU:0, one launch (start us, length us, event | category | flops | bytes accessed | tf_op | source)
XLA Modules:
  0.0 244.2 jit_solution(14877845565657748653)
XLA Ops:
  8.4 1.2 fusion.39
  9.6 1.9 fusion.41.x_ref
  11.6 56.4 %shard_map.136 = bf16[8,128,1280]{2,1,0:T(8,128)(2,1)} custom-call(bf16[128,1280]{1,0:T(8,128)(2,1)} %fusion.41.x_ref), custom_call_target="tpu_custom_call" | custom-call | bytes 70000000 | tf_op jit(solution)/shard_map/pallas_call | solution.py:242
  68.0 1.7 multiply_convert_fusion.key_ref.value_ref
  69.7 10.5 %shard_map.139 = f32[8,520,256]{2,1,0:T(8,128)} custom-call(bf16[1024,1024]{1,0:T(8,128)(2,1)} %rows_ref.1, bf16[1024,1024]{1,0:T(8,128)(2,1)} %multiply_convert_fusion.key_ref.value_ref, bf16[1024,1024]{1,0:T(8,128)(2,1)} %multiply_convert_fusion.key_ref.value_ref), custom_call_target="tpu_custom_call" | custom-call | flops 2147483648 | bytes 10485760 | tf_op jit(solution)/shard_map/pallas_call | solution.py:304
  81.1 2.0 fusion
  84.3 3.2 %convolution_convert_fusion = bf16[1024,480]{0,1:T(8,128)(2,1)S(1)} fusion(bf16[1024,1280]{1,0:T(8,128)(2,1)} %bitcast.55, bf16[1280,480]{0,1:T(8,128)(2,1)S(1)} %copy-done), kind=kOutput, calls=%fused_computation.23 | convolution fusion | flops 1258782720 | bytes 4833280 | tf_op jit(solution)/shard_map/dot_general | solution.py:377
  93.0 15.7 %shard_map.137 = bf16[8,160,128]{2,1,0:T(8,128)(2,1)} custom-call(bf16[8,160,128]{2,1,0:T(8,128)(2,1)} %bitcast_bitcast_fusion.refs_0_), custom_call_target="tpu_custom_call" | custom-call | bytes 30000000 | tf_op jit(solution)/shard_map/pallas_call | solution.py:109
  108.7 2.8 %fusion.60 = (f32[128]{0:T(128)S(1)}, f32[128,1280]{1,0:T(8,128)S(1)}) fusion(bf16[1280,128]{1,0:T(8,128)(2,1)} %bitcast.57, bf16[1280,1280]{1,0:T(8,128)(2,1)} %all-gather.3.cloned.1.call-done, bf16[128,1280]{1,0:T(8,128)(2,1)S(1)} %copy-done.2), kind=kOutput, calls=%fused_computation.91 | convolution fusion | flops 419921792 | bytes 4588032 | tf_op jit(solution)/shard_map/dp,de->pe/dot_general | solution.py:381
  112.8 45.4 %shard_map.138 = bf16[8,32,5120]{2,1,0:T(8,128)(2,1)} custom-call(bf16[32,5120]{1,0:T(8,128)(2,1)} %reshape.132.x_ref), custom_call_target="tpu_custom_call" | custom-call | bytes 70000000 | tf_op jit(solution)/shard_map/pallas_call | solution.py:242
  159.0 1.9 fusion.42
  161.9 8.4 %convolution_convert_fusion.1.rows_ref = bf16[256,1024]{1,0:T(8,128)(2,1)} fusion(bf16[256,5120]{1,0:T(8,128)(2,1)} %bitcast.56, bf16[5120,1024]{1,0:T(8,128)(2,1)} %param.19), kind=kOutput, calls=%fused_computation.24 | convolution fusion | flops 2684616704 | bytes 13631488 | tf_op jit(solution)/shard_map/dot_general | solution.py:389
  170.3 7.2 %shard_map.140 = (bf16[8,128,256]{2,1,0:T(8,128)(2,1)}, f32[8,8,128]{2,1,0:T(8,128)}) custom-call(bf16[256,1024]{1,0:T(8,128)(2,1)} %convolution_convert_fusion.1.rows_ref, bf16[1024,1024]{1,0:T(8,128)(2,1)} %multiply_convert_fusion.key_ref.value_ref, bf16[1024,1024]{1,0:T(8,128)(2,1)} %multiply_convert_fusion.key_ref.value_ref), custom_call_target="tpu_custom_call" | custom-call | flops 536870912 | bytes 2621440 | tf_op jit(solution)/shard_map/pallas_call | solution.py:304
  177.5 14.1 %shard_map.141 = (bf16[8,128,256]{2,1,0:T(8,128)(2,1)}, f32[8,8,128]{2,1,0:T(8,128)}) custom-call(bf16[8,128,256]{2,1,0:T(8,128)(2,1)} %get-tuple-element.19.refs_0_, f32[8,8,128]{2,1,0:T(8,128)} %get-tuple-element.20.refs_1_), custom_call_target="tpu_custom_call" | custom-call | bytes 30000000 | tf_op jit(solution)/shard_map/pallas_call | solution.py:109
  192.4 1.1 convert_reduce_fusion
  194.3 11.4 %shard_map.142 = bf16[8,128,256]{2,1,0:T(8,128)(2,1)} custom-call(bf16[128,256]{1,0:T(8,128)(2,1)} %multiply_convert_fusion.2.refs_0_), custom_call_target="tpu_custom_call" | custom-call | bytes 30000000 | tf_op jit(solution)/shard_map/pallas_call | solution.py:109
  205.7 1.5 multiply_reduce_fusion.2
  207.2 1.7 fusion.59
  208.9 2.0 fusion.61
  210.9 2.6 %fusion.1 = (f32[512]{0:T(512)S(1)}, bf16[512,4224]{1,0:T(8,128)(2,1)S(1)}) fusion(f32[512,4224]{1,0:T(8,128)S(1)} %get-tuple-element.38, f32[512]{0:T(512)S(1)} %get-tuple-element.37, pred[128,4224]{1,0:T(8,128)(4,1)S(1)} %pad_add_fusion), kind=kLoop, calls=%fused_computation.4 | loop fusion | flops 8650240 | bytes 13520896 | tf_op jit(solution)/shard_map/reduce_sum | solution.py:423
  214.0 1.3 convolution_multiply_fusion
  216.7 18.0 %shard_map.143 = bf16[8,128,512]{2,1,0:T(8,128)(2,1)} custom-call(bf16[128,512]{1,0:T(8,128)(2,1)} %bitcast.62), custom_call_target="tpu_custom_call" | custom-call | bytes 70000000 | tf_op jit(solution)/shard_map/pallas_call | solution.py:242
  234.7 1.6 copy.30
  236.3 1.3 copy.31
  (65 shorter events, 15.0 us)
Async XLA Ops:
  6.5 77.7 %copy-start = (bf16[1280,480]{0,1:T(8,128)(2,1)S(1)}, bf16[1280,480]{0,1:T(8,128)(2,1)}, u32[]{:S(2)}) copy-start(bf16[1280,480]{0,1:T(8,128)(2,1)} %param.16) | copy-start | bytes 3686404
  6.5 61.4 %copy-start.3 = (bf16[1024,1024]{1,0:T(8,128)(2,1)S(1)}, bf16[1024,1024]{1,0:T(8,128)(2,1)}, u32[]{:S(2)}) copy-start(bf16[1024,1024]{1,0:T(8,128)(2,1)} %param.24) | copy-start | bytes 6291460
  6.5 61.5 %copy-start.6 = (f32[1024]{0:T(1024)S(1)}, f32[1024]{0:T(1024)}, u32[]{:S(2)}) copy-start(f32[1024]{0:T(1024)} %param.23) | copy-start | bytes 12292
  6.5 63.2 %all-gather.3.cloned.1.call-start = ((), (), s32[]{:S(2)}) async-start(), calls=%async_computation.1 | async-start | bytes 3686400 | tf_op jit(solution)/shard_map/all_gather | solution.py:369
  7.3 151.0 %reduce-scatter.2.cloned.1.call-start = ((), (), s32[]{:S(2)}) async-start(), calls=%async_computation.2 | async-start | bytes 4792320 | tf_op jit(solution)/shard_map/reduce_scatter | solution.py:373
  80.3 0.8 copy-start.7
  80.3 0.8 copy-start.8
  80.3 126.9 %all-gather.5.cloned.1.call-start = ((), (), s32[]{:S(2)}) async-start(), calls=%async_computation.3 | async-start | bytes 2359296 | tf_op jit(solution)/shard_map/all_gather | solution.py:329
  91.3 17.4 %copy-start.2 = (bf16[128,1280]{1,0:T(8,128)(2,1)S(1)}, bf16[128,1280]{1,0:T(8,128)(2,1)}, u32[]{:S(2)}) copy-start(bf16[128,1280]{1,0:T(8,128)(2,1)} %param.14) | copy-start | bytes 983044
  92.2 19.5 %copy-start.5 = (f32[1280]{0:T(1024)S(1)}, f32[1280]{0:T(1024)}, u32[]{:S(2)}) copy-start(f32[1280]{0:T(1024)} %param.18) | copy-start | bytes 15364
  213.4 1.8 copy-start.4
  215.3 22.4 %copy-start.1 = (bf16[1280,480]{0,1:T(8,128)(2,1)S(1)}, bf16[1280,480]{0,1:T(8,128)(2,1)}, u32[]{:S(2)}) copy-start(bf16[1280,480]{0,1:T(8,128)(2,1)} %param.16) | copy-start | bytes 3686404
Sparse Core Ops, SparseCore 0:
  9.0 54.2 all-gather.2
  80.4 62.4 reduce-scatter.1
  161.0 27.2 all-gather.4

commit v4 on v3

--- a/solution.py
+++ b/solution.py
@@ -258,66 +258,66 @@
     )(x)
 
 
-def project_kernel(joined, rows_ref, key_ref, value_ref, out_ref, *rest):
-    sums_ref = rest[-1]
+def project_kernel(joined, rows_ref, weight_ref, out_ref, *rest):
     each = rows_ref.shape[0]
     rows = rows_ref[...]
-
-    @pl.when(pl.program_id(1) == 0)
-    def _():
-        floats = rows.astype(F32)
-        squares = floats * floats
-        coarse = squares.astype(BF16)
-        fine = (squares - coarse.astype(F32)).astype(BF16)
-        ones = jnp.ones((8, rows.shape[1]), BF16)
-        dims = (((1,), (1,)), ((), ()))
-        sums_ref[...] = lax.dot_general(
-            ones, coarse, dims, preferred_element_type=F32
-        ) + lax.dot_general(ones, fine, dims, preferred_element_type=F32)
-
-    both = jnp.concatenate([key_ref[...], value_ref[...]], axis=1)
-    raw = jnp.dot(rows, both, preferred_element_type=F32)
-    if joined:
-        out_ref[0, :each, :] = raw
-        out_ref[0, each:, :] = sums_ref[:, : 2 * HD]
-        for part in range(1, each // (2 * HD)):
-            out_ref[0, each + part : each + part + 1, :] = sums_ref[
-                :1, part * 2 * HD : (part + 1) * 2 * HD
-            ]
-    else:
-        out_ref[0] = raw.astype(BF16)
-        rest[0][0] = sums_ref[...]
+    floats = rows.astype(F32)
+    squares = floats * floats
+    coarse = squares.astype(BF16)
+    fine = (squares - coarse.astype(F32)).astype(BF16)
+    ones = jnp.ones((8, rows.shape[1]), BF16)
+    dims = (((1,), (1,)), ((), ()))
+    sums = lax.dot_general(ones, coarse, dims, preferred_element_type=F32)
+    sums += lax.dot_general(ones, fine, dims, preferred_element_type=F32)
+    for half in range(2):
+        for pair in range(KVH // 2):
+            first = (half * KVH + pair * 2) * HD
+            raw = jnp.dot(
+                rows, weight_ref[:, first : first + 2 * HD], preferred_element_type=F32
+            ).astype(out_ref.dtype)
+            for i in range(2):
+                out_ref[pair * 2 + i, 0, :each, half * HD : (half + 1) * HD] = raw[
+                    :, i * HD : (i + 1) * HD
+                ]
+    for h in range(KVH):
+        if joined:
+            out_ref[h, 0, each:, :] = sums[:, : 2 * HD]
+            for part in range(1, each // (2 * HD)):
+                out_ref[h, 0, each + part : each + part + 1, :] = sums[
+                    :1, part * 2 * HD : (part + 1) * 2 * HD
+                ]
+        else:
+            rest[0][h, 0] = sums
 
 
 def project(rows, weight, parts, joined):
     count, depth = rows.shape
     each = count // parts
-    pieces = KVH * parts
-    place = lambda p, h: (h * parts + p, 0, 0)
     if joined:
-        shapes = [jax.ShapeDtypeStruct((pieces, each + 8, 2 * HD), F32)]
+        shapes = [jax.ShapeDtypeStruct((KVH, parts, each + 8, 2 * HD), F32)]
     else:
         shapes = [
-            jax.ShapeDtypeStruct((pieces, each, 2 * HD), BF16),
-            jax.ShapeDtypeStruct((pieces, 8, each), F32),
+            jax.ShapeDtypeStruct((KVH, parts, each, 2 * HD), BF16),
+            jax.ShapeDtypeStruct((KVH, parts, 8, each), F32),
         ]
-    return pl.pallas_call(
+    outs = pl.pallas_call(
         functools.partial(project_kernel, joined),
-        grid=(parts, KVH),
+        grid=(parts,),
         out_shape=shapes,
         in_specs=[
-            pl.BlockSpec((each, depth), lambda p, h: (p, 0)),
-            pl.BlockSpec((depth, HD), lambda p, h: (0, h)),
-            pl.BlockSpec((depth, HD), lambda p, h: (0, KVH + h)),
+            pl.BlockSpec((each, depth), lambda p: (p, 0)),
+            pl.BlockSpec(weight.shape, lambda p: (0, 0)),
         ],
-        out_specs=[pl.BlockSpec((1,) + shape.shape[1:], place) for shape in shapes],
-        scratch_shapes=[pltpu.VMEM((8, each), F32)],
+        out_specs=[
+            pl.BlockSpec((KVH, 1) + shape.shape[2:], lambda p: (0, p, 0, 0)) for shape in shapes
+        ],
         cost_estimate=pl.CostEstimate(
             flops=2 * count * depth * KVH * 2 * HD,
             bytes_accessed=count * depth * 10,
             transcendentals=0,
         ),
-    )(rows, weight, weight)
+    )(rows, weight)
+    return [out.reshape((KVH * parts,) + out.shape[2:]) for out in outs]
 
 
 def whole_text(total):
@@ -366,7 +366,13 @@
     floats = patches.astype(F32)
     normed = layer_norm(floats, vis_gain).astype(BF16)
     gathered = line_gather(normed, 2, 0).reshape(-1, VD)
-    w_out_all = lax.all_gather(w_out, VIS, axis=0, tiled=True)
+    few = w_out.shape[0] // ctx_count
+    w_out_all = lax.all_gather(
+        lax.dynamic_slice_in_dim(w_out, lax.axis_index("ctx") * few, few, 0),
+        ("ctx",) + VIS,
+        axis=0,
+        tiled=True,
+    )
 
     weight = (w_kv.astype(F32) * kv_gain[:, None]).astype(BF16)
     weight, gathered, w_out_all = lax.optimization_barrier((weight, gathered, w_out_all))
@@ -378,6 +384,7 @@
     heads = vision_attention(qkv, local_heads)
     heads = heads.reshape(-1, vis_count, patch_count).transpose(1, 0, 2)
     (returned,) = exchange((heads,), VIS, False, 1)
+    returned = returned.reshape(vis_count, ctx_count, few, patch_count).transpose(1, 0, 2, 3)
     projected = jnp.einsum(
         "dp,de->pe", returned.reshape(VD, patch_count), w_out_all, preferred_element_type=F32
     )

time: 245 us -> 239 us (0.976)
  Pallas kernels: 179 us -> 146 us
  waiting for transfers between devices: 0.78 us -> 24.9 us
  local copies, waits for them, and re-layouts: 8.35 us -> 11 us
    pallas_call x3, Pallas kernels: 120 us -> 94.9 us  [line_gather(): pl.pallas_call(functools.partial(line_kernel, sizes, chunks), out_shape=j...]
    all_gather x1, waiting for transfers between devices: 0.01 us -> 24.8 us  [per_device(): lax.all_gather(lax.dynamic_slice_in_dim(w_out, lax.axis_index('ctx') * fe...]
    pallas_call x2, Pallas kernels: 17.8 us -> 10.5 us  [project(): pl.pallas_call(functools.partial(project_kernel, joined), grid=(parts,),...]
  transfers between devices with their start and end apart: 3 -> 3, of which waited for: 0 -> 1; matrix products, arithmetic and copies ran while one was open for 14% -> 15% of each run, Pallas kernels for 62% -> 51%
where the time goes in v4:
time: 239 us; the launch traced here: 238 us
  Pallas kernels  146 us (61%)
  waiting for transfers between devices  24.9 us (10%)
  matrix products  23 us (10%)
  other arithmetic  19.1 us (8%)
  between operations  14.1 us (6%)
  local copies, waits for them, and re-layouts  11 us (5%)
    pallas_call x3, Pallas kernels, line_gather(): pl.pallas_call(functools.partial(line_kernel, sizes, chunks), out_shape=j...  94.9 us
    pallas_call x3, Pallas kernels, exchange(): pl.pallas_call(functools.partial(exchange_kernel, names, sizes, spread, c...  40.5 us
    all_gather x1, waiting for transfers between devices, per_device(): lax.all_gather(lax.dynamic_slice_in_dim(w_out, lax.axis_index('ctx') * fe...  24.8 us
    pallas_call x2, Pallas kernels, project(): pl.pallas_call(functools.partial(project_kernel, joined), grid=(parts,),...  10.5 us
    dot_general x1, matrix products, per_device(): visual = jnp.dot(merged, w_merge, preferred_element_type=F32).astype(BF16)  8.44 us
  transfers between devices with their start and end apart: 3, of which 1 were waited for; matrix products, arithmetic and copies ran while one was open for 15% of the time, Pallas kernels for 51%

profile of v4, /device:TPU:0, one launch (start us, length us, event | category | flops | bytes accessed | tf_op | source)
XLA Modules:
  0.0 238.4 jit_solution(11517848230368303897)
XLA Ops:
  6.6 1.7 constant_dynamic-slice_fusion.2
  10.6 1.9 fusion.41.x_ref
  12.6 33.7 %shard_map.136 = bf16[8,128,1280]{2,1,0:T(8,128)(2,1)} custom-call(bf16[128,1280]{1,0:T(8,128)(2,1)} %fusion.41.x_ref), custom_call_target="tpu_custom_call" | custom-call | bytes 70000000 | tf_op jit(solution)/shard_map/pallas_call | solution.py:242
  46.3 1.7 multiply_convert_fusion.weight_ref
  48.0 24.8 %all-gather.3.cloned.1.call-done = bf16[1280,1280]{1,0:T(8,128)(2,1)} async-done(((bf16[40,1280]{1,0:T(8,128)(2,1)}), bf16[1280,1280]{1,0:T(8,128)(2,1)}) %all-gather.3.cloned.1.call-update) | async-done | bytes 3276816 | tf_op jit(solution)/shard_map/all_gather | solution.py:370
  72.9 7.0 %shard_map.139 = f32[4,2,520,256]{3,2,1,0:T(8,128)} custom-call(bf16[1024,1024]{1,0:T(8,128)(2,1)} %rows_ref.1, bf16[1024,1024]{1,0:T(8,128)(2,1)} %multiply_convert_fusion.weight_ref), custom_call_target="tpu_custom_call" | custom-call | flops 2147483648 | bytes 10485760 | tf_op jit(solution)/shard_map/pallas_call | solution.py:303
  80.8 2.0 fusion
  84.0 3.4 %convolution_convert_fusion = bf16[1024,480]{0,1:T(8,128)(2,1)S(1)} fusion(bf16[1024,1280]{1,0:T(8,128)(2,1)} %bitcast.62, bf16[1280,480]{0,1:T(8,128)(2,1)S(1)} %copy-done), kind=kOutput, calls=%fused_computation.23 | convolution fusion | flops 1258782720 | bytes 4833280 | tf_op jit(solution)/shard_map/dot_general | solution.py:383
  92.9 14.9 %shard_map.137 = bf16[8,160,128]{2,1,0:T(8,128)(2,1)} custom-call(bf16[8,160,128]{2,1,0:T(8,128)(2,1)} %bitcast_bitcast_fusion.refs_0_), custom_call_target="tpu_custom_call" | custom-call | bytes 30000000 | tf_op jit(solution)/shard_map/pallas_call | solution.py:109
  108.9 2.7 %fusion.60 = (f32[128]{0:T(128)S(1)}, f32[128,1280]{1,0:T(8,128)S(1)}) fusion(bf16[1280,128]{1,0:T(8,128)(2,1)S(1)} %bitcast.64, bf16[1280,1280]{1,0:T(8,128)(2,1)} %all-gather.3.cloned.1.call-done, bf16[128,1280]{1,0:T(8,128)(2,1)S(1)} %copy-done.2), kind=kOutput, calls=%fused_computation.92 | convolution fusion | flops 419921792 | bytes 4588032 | tf_op jit(solution)/shard_map/dp,de->pe/dot_general | solution.py:388
  112.9 43.4 %shard_map.138 = bf16[8,32,5120]{2,1,0:T(8,128)(2,1)} custom-call(bf16[32,5120]{1,0:T(8,128)(2,1)} %reshape.145.x_ref), custom_call_target="tpu_custom_call" | custom-call | bytes 70000000 | tf_op jit(solution)/shard_map/pallas_call | solution.py:242
  157.0 1.9 fusion.42
  159.9 8.4 %convolution_convert_fusion.1.rows_ref = bf16[256,1024]{1,0:T(8,128)(2,1)} fusion(bf16[256,5120]{1,0:T(8,128)(2,1)} %bitcast.63, bf16[5120,1024]{1,0:T(8,128)(2,1)} %param.19), kind=kOutput, calls=%fused_computation.24 | convolution fusion | flops 2684616704 | bytes 13631488 | tf_op jit(solution)/shard_map/dot_general | solution.py:396
  168.4 3.6 %shard_map.140 = (bf16[4,2,128,256]{3,2,1,0:T(8,128)(2,1)}, f32[4,2,8,128]{3,2,1,0:T(8,128)}) custom-call(bf16[256,1024]{1,0:T(8,128)(2,1)} %convolution_convert_fusion.1.rows_ref, bf16[1024,1024]{1,0:T(8,128)(2,1)} %multiply_convert_fusion.weight_ref), custom_call_target="tpu_custom_call" | custom-call | flops 536870912 | bytes 2621440 | tf_op jit(solution)/shard_map/pallas_call | solution.py:303
  171.9 14.1 %shard_map.141 = (bf16[8,128,256]{2,1,0:T(8,128)(2,1)}, f32[8,8,128]{2,1,0:T(8,128)}) custom-call(bf16[8,128,256]{2,1,0:T(8,128)(2,1)} %bitcast.71, f32[8,8,128]{2,1,0:T(8,128)} %bitcast.75), custom_call_target="tpu_custom_call" | custom-call | bytes 30000000 | tf_op jit(solution)/shard_map/pallas_call | solution.py:109
  188.7 11.4 %shard_map.142 = bf16[8,128,256]{2,1,0:T(8,128)(2,1)} custom-call(bf16[128,256]{1,0:T(8,128)(2,1)} %multiply_convert_fusion.2.refs_0_), custom_call_target="tpu_custom_call" | custom-call | bytes 30000000 | tf_op jit(solution)/shard_map/pallas_call | solution.py:109
  200.1 1.5 multiply_reduce_fusion.2
  201.6 1.7 fusion.59
  203.3 2.0 fusion.61
  205.3 2.6 %fusion.1 = (f32[512]{0:T(512)S(1)}, bf16[512,4224]{1,0:T(8,128)(2,1)S(1)}) fusion(f32[512,4224]{1,0:T(8,128)S(1)} %get-tuple-element.38, f32[512]{0:T(512)S(1)} %get-tuple-element.37, pred[128,4224]{1,0:T(8,128)(4,1)S(1)} %pad_add_fusion), kind=kLoop, calls=%fused_computation.4 | loop fusion | flops 8650240 | bytes 13520896 | tf_op jit(solution)/shard_map/reduce_sum | solution.py:430
  208.4 1.3 convolution_multiply_fusion
  211.1 17.9 %shard_map.143 = bf16[8,128,512]{2,1,0:T(8,128)(2,1)} custom-call(bf16[128,512]{1,0:T(8,128)(2,1)} %bitcast.70), custom_call_target="tpu_custom_call" | custom-call | bytes 70000000 | tf_op jit(solution)/shard_map/pallas_call | solution.py:242
  228.9 1.6 copy.33
  230.6 1.3 copy.34
  (67 shorter events, 17.9 us)
Async XLA Ops:
  6.5 77.5 %copy-start = (bf16[1280,480]{0,1:T(8,128)(2,1)S(1)}, bf16[1280,480]{0,1:T(8,128)(2,1)}, u32[]{:S(2)}) copy-start(bf16[1280,480]{0,1:T(8,128)(2,1)} %param.16) | copy-start | bytes 3686404
  6.5 39.7 %copy-start.3 = (bf16[1024,1024]{1,0:T(8,128)(2,1)S(1)}, bf16[1024,1024]{1,0:T(8,128)(2,1)}, u32[]{:S(2)}) copy-start(bf16[1024,1024]{1,0:T(8,128)(2,1)} %param.24) | copy-start | bytes 6291460
  6.5 39.7 %copy-start.6 = (f32[1024]{0:T(1024)S(1)}, f32[1024]{0:T(1024)}, u32[]{:S(2)}) copy-start(f32[1024]{0:T(1024)} %param.23) | copy-start | bytes 12292
  6.5 66.3 %all-gather.3.cloned.1.call-start = ((), (), s32[]{:S(2)}) async-start(), calls=%async_computation.1 | async-start | bytes 3379200 | tf_op jit(solution)/shard_map/all_gather | solution.py:370
  8.3 148.0 %reduce-scatter.2.cloned.1.call-start = ((), (), s32[]{:S(2)}) async-start(), calls=%async_computation.2 | async-start | bytes 4792320 | tf_op jit(solution)/shard_map/reduce_scatter | solution.py:379
  79.8 0.9 copy-start.7
  79.8 0.9 copy-start.8
  79.9 121.8 %all-gather.5.cloned.1.call-start = ((), (), s32[]{:S(2)}) async-start(), calls=%async_computation.3 | async-start | bytes 2359296 | tf_op jit(solution)/shard_map/all_gather | solution.py:329
  91.2 17.6 %copy-start.2 = (bf16[128,1280]{1,0:T(8,128)(2,1)S(1)}, bf16[128,1280]{1,0:T(8,128)(2,1)}, u32[]{:S(2)}) copy-start(bf16[128,1280]{1,0:T(8,128)(2,1)} %param.14) | copy-start | bytes 983044
  92.1 19.7 %copy-start.5 = (f32[1280]{0:T(1024)S(1)}, f32[1280]{0:T(1024)}, u32[]{:S(2)}) copy-start(f32[1280]{0:T(1024)} %param.18) | copy-start | bytes 15364
  207.9 1.8 copy-start.4
  209.7 22.2 %copy-start.1 = (bf16[1280,480]{0,1:T(8,128)(2,1)S(1)}, bf16[1280,480]{0,1:T(8,128)(2,1)}, u32[]{:S(2)}) copy-start(bf16[1280,480]{0,1:T(8,128)(2,1)} %param.16) | copy-start | bytes 3686404
Sparse Core Ops, SparseCore 0:
  10.2 62.6 all-gather.2
  80.0 61.4 reduce-scatter.1
  159.0 27.0 all-gather.4

commit v5 on v4

--- a/solution.py
+++ b/solution.py
@@ -375,15 +375,15 @@
     )
 
     weight = (w_kv.astype(F32) * kv_gain[:, None]).astype(BF16)
-    weight, gathered, w_out_all = lax.optimization_barrier((weight, gathered, w_out_all))
-    text_total = lax.psum_scatter(
-        project(prompt_text, weight, parts, True)[0], VIS, scatter_dimension=0, tiled=True
-    )
 
     qkv = jnp.dot(gathered, w_qkv, preferred_element_type=F32).astype(BF16)
     heads = vision_attention(qkv, local_heads)
     heads = heads.reshape(-1, vis_count, patch_count).transpose(1, 0, 2)
     (returned,) = exchange((heads,), VIS, False, 1)
+    weight, returned, w_out_all = lax.optimization_barrier((weight, returned, w_out_all))
+    text_total = lax.psum_scatter(
+        project(prompt_text, weight, parts, True)[0], VIS, scatter_dimension=0, tiled=True
+    )
     returned = returned.reshape(vis_count, ctx_count, few, patch_count).transpose(1, 0, 2, 3)
     projected = jnp.einsum(
         "dp,de->pe", returned.reshape(VD, patch_count), w_out_all, preferred_element_type=F32
@@ -391,9 +391,9 @@
     mixed = floats + projected
     merged = layer_norm(mixed, merge_gain).astype(BF16).reshape(patch_count // 4, MD)
     merged = line_gather(merged, 2, 2).reshape(-1, MD)
-    merged, text_total = lax.optimization_barrier((merged, text_total))
+    visual = jnp.dot(merged, w_merge, preferred_element_type=F32).astype(BF16)
+    visual, text_total = lax.optimization_barrier((visual, text_total))
     text_kv = whole_text(text_total)
-    visual = jnp.dot(merged, w_merge, preferred_element_type=F32).astype(BF16)
     image_kv = whole_image(visual, weight, parts)
 
     flat = (token_dest * shard_rows + token_row).reshape(-1)

time: 239 us -> 233 us (0.975)
  waiting for transfers between devices: 24.9 us -> 7.82 us
  Pallas kernels: 146 us -> 157 us
    all_gather x1, waiting for transfers between devices: 24.8 us -> 5.98 us  [per_device(): lax.all_gather(lax.dynamic_slice_in_dim(w_out, lax.axis_index('ctx') * fe...]
    pallas_call x3, Pallas kernels: 94.9 us -> 106 us  [line_gather(): pl.pallas_call(functools.partial(line_kernel, sizes, chunks), out_shape=j...]
  transfers between devices with their start and end apart: 3 -> 3, of which waited for: 1 -> 2; matrix products, arithmetic and copies ran while one was open for 15% -> 15% of each run, Pallas kernels for 51% -> 57%
where the time goes in v5:
time: 233 us; the launch traced here: 232 us
  Pallas kernels  157 us (67%)
  matrix products  22.9 us (10%)
  other arithmetic  19.4 us (8%)
  between operations  14.1 us (6%)
  local copies, waits for them, and re-layouts  11 us (5%)
  waiting for transfers between devices  7.82 us (3%)
    pallas_call x3, Pallas kernels, line_gather(): pl.pallas_call(functools.partial(line_kernel, sizes, chunks), out_shape=j...  106 us
    pallas_call x3, Pallas kernels, exchange(): pl.pallas_call(functools.partial(exchange_kernel, names, sizes, spread, c...  40.1 us
    pallas_call x2, Pallas kernels, project(): pl.pallas_call(functools.partial(project_kernel, joined), grid=(parts,),...  10.5 us
    dot_general x1, matrix products, per_device(): visual = jnp.dot(merged, w_merge, preferred_element_type=F32).astype(BF16)  8.56 us
    all_gather x1, waiting for transfers between devices, per_device(): lax.all_gather(lax.dynamic_slice_in_dim(w_out, lax.axis_index('ctx') * fe...  5.98 us
  transfers between devices with their start and end apart: 3, of which 2 were waited for; matrix products, arithmetic and copies ran while one was open for 15% of the time, Pallas kernels for 57%

profile of v5, /device:TPU:0, one launch (start us, length us, event | category | flops | bytes accessed | tf_op | source)
XLA Modules:
  0.0 231.9 jit_solution(11086953934012513014)
XLA Ops:
  6.5 1.6 constant_dynamic-slice_fusion.2
  10.6 1.9 fusion.41.x_ref
  12.5 33.7 %shard_map.136 = bf16[8,128,1280]{2,1,0:T(8,128)(2,1)} custom-call(bf16[128,1280]{1,0:T(8,128)(2,1)} %fusion.41.x_ref), custom_call_target="tpu_custom_call" | custom-call | bytes 70000000 | tf_op jit(solution)/shard_map/pallas_call | solution.py:242
  46.2 3.2 %convolution_convert_fusion = bf16[1024,480]{0,1:T(8,128)(2,1)S(1)} fusion(bf16[1024,1280]{1,0:T(8,128)(2,1)} %bitcast.62, bf16[1280,480]{0,1:T(8,128)(2,1)S(1)} %copy-done), kind=kOutput, calls=%fused_computation.23 | convolution fusion | flops 1258782720 | bytes 4833280 | tf_op jit(solution)/shard_map/dot_general | solution.py:379
  54.9 13.7 %shard_map.137 = bf16[8,160,128]{2,1,0:T(8,128)(2,1)} custom-call(bf16[8,160,128]{2,1,0:T(8,128)(2,1)} %bitcast_bitcast_fusion.refs_0_), custom_call_target="tpu_custom_call" | custom-call | bytes 30000000 | tf_op jit(solution)/shard_map/pallas_call | solution.py:109
  68.6 1.8 multiply_convert_fusion.weight_ref
  70.4 6.0 %all-gather.3.cloned.1.call-done = bf16[1280,1280]{1,0:T(8,128)(2,1)} async-done(((bf16[40,1280]{1,0:T(8,128)(2,1)}), bf16[1280,1280]{1,0:T(8,128)(2,1)}) %all-gather.3.cloned.1.call-update) | async-done | bytes 3276816 | tf_op jit(solution)/shard_map/all_gather | solution.py:370
  76.4 7.0 %shard_map.139 = f32[4,2,520,256]{3,2,1,0:T(8,128)} custom-call(bf16[1024,1024]{1,0:T(8,128)(2,1)} %rows_ref.1, bf16[1024,1024]{1,0:T(8,128)(2,1)} %multiply_convert_fusion.weight_ref), custom_call_target="tpu_custom_call" | custom-call | flops 2147483648 | bytes 10485760 | tf_op jit(solution)/shard_map/pallas_call | solution.py:303
  84.4 2.6 %fusion.60 = (f32[128]{0:T(128)S(1)}, f32[128,1280]{1,0:T(8,128)S(1)}) fusion(bf16[1280,128]{1,0:T(8,128)(2,1)S(1)} %bitcast.64, bf16[1280,1280]{1,0:T(8,128)(2,1)} %all-gather.3.cloned.1.call-done, bf16[128,1280]{1,0:T(8,128)(2,1)S(1)} %copy-done.2), kind=kOutput, calls=%fused_computation.92 | convolution fusion | flops 419921792 | bytes 4588032 | tf_op jit(solution)/shard_map/dp,de->pe/dot_general | solution.py:388
  88.4 53.8 %shard_map.138 = bf16[8,32,5120]{2,1,0:T(8,128)(2,1)} custom-call(bf16[32,5120]{1,0:T(8,128)(2,1)} %reshape.145.x_ref), custom_call_target="tpu_custom_call" | custom-call | bytes 70000000 | tf_op jit(solution)/shard_map/pallas_call | solution.py:242
  142.3 8.6 %convolution_convert_fusion.1.rows_ref = bf16[256,1024]{1,0:T(8,128)(2,1)} fusion(bf16[256,5120]{1,0:T(8,128)(2,1)} %bitcast.63, bf16[5120,1024]{1,0:T(8,128)(2,1)} %param.19), kind=kOutput, calls=%fused_computation.24 | convolution fusion | flops 2684616704 | bytes 13631488 | tf_op jit(solution)/shard_map/dot_general | solution.py:394
  150.8 1.8 reduce-scatter.2.cloned.1.call-done
  153.3 1.9 fusion.42
  156.0 2.0 fusion
  160.2 3.6 %shard_map.140 = (bf16[4,2,128,256]{3,2,1,0:T(8,128)(2,1)}, f32[4,2,8,128]{3,2,1,0:T(8,128)}) custom-call(bf16[256,1024]{1,0:T(8,128)(2,1)} %convolution_convert_fusion.1.rows_ref, bf16[1024,1024]{1,0:T(8,128)(2,1)} %multiply_convert_fusion.weight_ref), custom_call_target="tpu_custom_call" | custom-call | flops 536870912 | bytes 2621440 | tf_op jit(solution)/shard_map/pallas_call | solution.py:303
  163.7 15.0 %shard_map.141 = (bf16[8,128,256]{2,1,0:T(8,128)(2,1)}, f32[8,8,128]{2,1,0:T(8,128)}) custom-call(bf16[8,128,256]{2,1,0:T(8,128)(2,1)} %bitcast.71, f32[8,8,128]{2,1,0:T(8,128)} %bitcast.75), custom_call_target="tpu_custom_call" | custom-call | bytes 30000000 | tf_op jit(solution)/shard_map/pallas_call | solution.py:109
  181.3 11.5 %shard_map.142 = bf16[8,128,256]{2,1,0:T(8,128)(2,1)} custom-call(bf16[128,256]{1,0:T(8,128)(2,1)} %multiply_convert_fusion.2.refs_0_), custom_call_target="tpu_custom_call" | custom-call | bytes 30000000 | tf_op jit(solution)/shard_map/pallas_call | solution.py:109
  192.8 1.5 multiply_reduce_fusion.2
  194.3 1.7 fusion.59
  196.0 2.0 fusion.61
  198.0 2.8 %fusion.1 = (f32[512]{0:T(512)S(1)}, bf16[512,4224]{1,0:T(8,128)(2,1)S(1)}) fusion(f32[512,4224]{1,0:T(8,128)S(1)} %get-tuple-element.38, f32[512]{0:T(512)S(1)} %get-tuple-element.37, pred[128,4224]{1,0:T(8,128)(4,1)S(1)} %pad_add_fusion), kind=kLoop, calls=%fused_computation.4 | loop fusion | flops 8650240 | bytes 13520896 | tf_op jit(solution)/shard_map/reduce_sum | solution.py:430
  204.0 18.5 %shard_map.143 = bf16[8,128,512]{2,1,0:T(8,128)(2,1)} custom-call(bf16[128,512]{1,0:T(8,128)(2,1)} %bitcast.70), custom_call_target="tpu_custom_call" | custom-call | bytes 70000000 | tf_op jit(solution)/shard_map/pallas_call | solution.py:242
  222.5 1.6 copy.33
  224.1 1.3 copy.34
  (69 shorter events, 19.0 us)
Async XLA Ops:
  6.5 39.6 %copy-start = (bf16[1280,480]{0,1:T(8,128)(2,1)S(1)}, bf16[1280,480]{0,1:T(8,128)(2,1)}, u32[]{:S(2)}) copy-start(bf16[1280,480]{0,1:T(8,128)(2,1)} %param.16) | copy-start | bytes 3686404
  6.5 69.9 %all-gather.3.cloned.1.call-start = ((), (), s32[]{:S(2)}) async-start(), calls=%async_computation.1 | async-start | bytes 3379200 | tf_op jit(solution)/shard_map/all_gather | solution.py:370
  8.2 144.4 %reduce-scatter.2.cloned.1.call-start = ((), (), s32[]{:S(2)}) async-start(), calls=%async_computation.2 | async-start | bytes 4792320 | tf_op jit(solution)/shard_map/reduce_scatter | solution.py:384
  53.3 15.3 %copy-start.3 = (bf16[1024,1024]{1,0:T(8,128)(2,1)S(1)}, bf16[1024,1024]{1,0:T(8,128)(2,1)}, u32[]{:S(2)}) copy-start(bf16[1024,1024]{1,0:T(8,128)(2,1)} %param.24) | copy-start | bytes 6291460
  53.3 15.3 %copy-start.7 = (f32[1024]{0:T(1024)S(1)}, f32[1024]{0:T(1024)}, u32[]{:S(2)}) copy-start(f32[1024]{0:T(1024)} %param.23) | copy-start | bytes 12292
  83.4 1.0 copy-start.4
  83.4 1.1 copy-start.2
  83.4 4.0 %copy-start.6 = (f32[1280]{0:T(1024)S(1)}, f32[1280]{0:T(1024)}, u32[]{:S(2)}) copy-start(f32[1280]{0:T(1024)} %param.18) | copy-start | bytes 15364
  83.4 110.9 %all-gather.5.cloned.1.call-start = ((), (), s32[]{:S(2)}) async-start(), calls=%async_computation.3 | async-start | bytes 2359296 | tf_op jit(solution)/shard_map/all_gather | solution.py:329
  142.3 13.7 %copy-start.8 = (s32[4,256]{1,0:T(4,128)S(1)}, s32[4,256]{1,0:T(4,128)}, u32[]{:S(2)}) copy-start(s32[4,256]{1,0:T(4,128)} %param.21) | copy-start | bytes 12292
  142.3 13.7 %copy-start.9 = (s32[4,256]{1,0:T(4,128)S(1)}, s32[4,256]{1,0:T(4,128)}, u32[]{:S(2)}) copy-start(s32[4,256]{1,0:T(4,128)} %param.20) | copy-start | bytes 12292
  200.8 1.8 copy-start.5
  202.6 22.8 %copy-start.1 = (bf16[1280,480]{0,1:T(8,128)(2,1)S(1)}, bf16[1280,480]{0,1:T(8,128)(2,1)}, u32[]{:S(2)}) copy-start(bf16[1280,480]{0,1:T(8,128)(2,1)} %param.16) | copy-start | bytes 3686404
Sparse Core Ops, SparseCore 0:
  10.2 66.1 all-gather.2
  83.5 69.0 reduce-scatter.1
  155.4 28.4 all-gather.4
